TPU v7x, 128 devices: a whole 4x4x4 slice. The times are simulated.
128 devices in a mesh: member: 16 (over x_lo, y, core), lon: 8 (over x_hi, z).
Axes of the slice: x: 4 (x_hi: 2, x_lo: 2; x = x_hi * 2 + x_lo), y: 4, z: 4, core: 2. Of those that a mesh axis runs over, the one named last changes fastest.
Arguments:
- atmos: bfloat16 [16, 96, 96, 1024], P('member', None, None, 'lon'), may hold values from -6 to 6
- ocean: bfloat16 [96, 96, 1024], P(None, None, 'lon'), may hold values from -6 to 6
- land_mask: int32 [96, 1024], P(None, 'lon'), may hold values 0 or 1
- ice_mask: int32 [96, 1024], P(None, 'lon'), may hold values 0 or 1
- atm_kernel: float32 [2, 7, 7, 96], replicated, may hold values from -0.875 to 0.875
- atm_gain: float32 [2, 96], replicated, may hold values from 0.25 to 1.75
- atm_up: bfloat16 [2, 96, 384], replicated, may hold values from -0.625 to 0.625
- atm_down: bfloat16 [2, 384, 96], replicated, may hold values from -0.3125 to 0.3125
- atm_scale: float32 [2, 96], replicated, may hold values from 0.5 to 1.5
- flux_weight: bfloat16 [96, 32], replicated, may hold values from -0.625 to 0.625
- flux_lift: bfloat16 [2, 32, 96], replicated, may hold values from -1 to 1
- ocn_kernel: float32 [7, 7, 96], replicated, may hold values from -0.875 to 0.875
- ocn_gain: float32 [96], replicated, may hold values from 0.25 to 1.75
- ocn_up: bfloat16 [96, 384], replicated, may hold values from -0.625 to 0.625
- ocn_down: bfloat16 [384, 96], replicated, may hold values from -0.3125 to 0.3125
- ocn_scale: float32 [96], replicated, may hold values from 0.5 to 1.5
- surf_weight: bfloat16 [96, 8], replicated, may hold values from -0.625 to 0.625
- back_weight: bfloat16 [8, 96], replicated, may hold values from -2 to 2
Outputs:
- atmos_out: bfloat16 [16, 96, 96, 1024], P('member', None, None, 'lon')
- ocean_new: bfloat16 [96, 96, 1024], P('member', None, 'lon')
All inputs are finite; a program needn't handle non-finite values. No bound on the sum of `land_mask` or of `ice_mask` on one device may be relied on, other than what follows from the above.
Results may differ from a plain program's by a relative error of at most 0.017.
Values may be sent and summed in bfloat16 or wider, within the bound.
A program may use at most 64 MiB of HBM per device.

v0:
```python
import jax
import jax.numpy as jnp
from jax import lax
from jax.sharding import PartitionSpec as P


def with_halo(cells, sides, width):
    for axis, dim in sides:
        count = lax.axis_size(axis)
        head = lax.slice_in_dim(cells, 0, width, axis=dim)
        tail = lax.slice_in_dim(cells, cells.shape[dim] - width, cells.shape[dim], axis=dim)
        cells = jnp.concatenate(
            [
                lax.ppermute(tail, axis, [(i, (i + 1) % count) for i in range(count)]),
                cells,
                lax.ppermute(head, axis, [((i + 1) % count, i) for i in range(count)]),
            ],
            axis=dim,
        )
    return cells


def contract(form, left, right):
    return jnp.einsum(form, left.astype(jnp.float32), right.astype(jnp.float32))


def mixer(field, padded, kernel, gain, up_proj, down_proj, scale, keep):
    rows = field.shape[0]
    cols = field.shape[2]
    acc = jnp.zeros(field.shape, jnp.float32)
    for i in range(7):
        for j in range(7):
            acc = (
                acc
                + padded[i : i + rows, :, j : j + cols].astype(jnp.float32) * kernel[i, j][:, None]
            )
    center = acc - jnp.mean(acc, axis=1, keepdims=True)
    spread = jnp.mean(center * center, axis=1, keepdims=True)
    normed = (center * lax.rsqrt(spread + 1e-06) * gain[:, None]).astype(jnp.bfloat16)
    hidden = jax.nn.gelu(contract("lcw,ch->lhw", normed, up_proj)).astype(jnp.bfloat16)
    branch = contract("lhw,hc->lcw", hidden, down_proj)
    result = field.astype(jnp.float32) + scale[:, None] * branch
    if keep is not None:
        result = result * keep[:, None, :]
    return result.astype(jnp.bfloat16)


def atmos_pad(state):
    tall = jnp.pad(state, ((3, 3), (0, 0), (0, 0)))
    return with_halo(tall, (("lon", 2),), 3)


def forced(ocean_part, flux_sum, count, sea, ice, flux_lift):
    flux_low = (flux_sum / count).astype(jnp.bfloat16)
    open_term = contract("lfw,fc->lcw", flux_low, flux_lift[0])
    ice_term = contract("lfw,fc->lcw", flux_low, flux_lift[1])
    forcing = sea[:, None, :] * ((1.0 - ice)[:, None, :] * open_term + ice[:, None, :] * ice_term)
    return (ocean_part.astype(jnp.float32) + forcing).astype(jnp.bfloat16)


def local(
    atmos,
    ocean,
    land_mask,
    ice_mask,
    atm_kernel,
    atm_gain,
    atm_up,
    atm_down,
    atm_scale,
    flux_weight,
    flux_lift,
    ocn_kernel,
    ocn_gain,
    ocn_up,
    ocn_down,
    ocn_scale,
    surf_weight,
    back_weight,
):
    sea = (1 - land_mask).astype(jnp.float32)
    ice = ice_mask.astype(jnp.float32)
    state = atmos[0]
    for layer in range(2):
        state = mixer(
            state,
            atmos_pad(state),
            atm_kernel[layer],
            atm_gain[layer],
            atm_up[layer],
            atm_down[layer],
            atm_scale[layer],
            None,
        )
    flux = jax.nn.gelu(contract("lcw,cf->lfw", state, flux_weight))
    members = lax.axis_size("member")
    rank = lax.axis_index("member")
    rows = state.shape[0] // members
    flux_sum = lax.psum(flux.astype(jnp.bfloat16), "member").astype(jnp.float32)
    ocean_mid = forced(ocean, flux_sum, members, sea, ice, flux_lift)
    tall = jnp.pad(ocean_mid, ((3, 3), (0, 0), (0, 0)))
    padded = with_halo(tall, (("lon", 2),), 3)
    ocean_full = mixer(ocean_mid, padded, ocn_kernel, ocn_gain, ocn_up, ocn_down, ocn_scale, sea)
    surface = contract("lcw,cs->lsw", ocean_full, surf_weight).astype(jnp.bfloat16)
    ocean_rows = lax.dynamic_slice_in_dim(ocean_full, rank * rows, rows, 0)
    coupling = sea[:, None, :] * contract("lsw,sc->lcw", surface, back_weight)
    atmos_out = (state.astype(jnp.float32) + coupling).astype(jnp.bfloat16)[None]
    return (atmos_out, ocean_rows)


def solution(mesh):
    in_specs = (
        P("member", None, None, "lon"),
        P(None, None, "lon"),
        P(None, "lon"),
        P(None, "lon"),
        P(),
        P(),
        P(),
        P(),
        P(),
        P(),
        P(),
        P(),
        P(),
        P(),
        P(),
        P(),
        P(),
        P(),
    )
    out_specs = (P("member", None, None, "lon"), P("member", None, "lon"))
    return jax.shard_map(local, mesh=mesh, in_specs=in_specs, out_specs=out_specs, check_vma=False)
```

profile of v0, /device:TPU:1, one launch (start us, length us, event | category | flops | bytes accessed | tf_op | source)
XLA Modules:
  0.0 510.7 jit_solution(5957040996771305564)
XLA Ops:
  7.2 0.0 copy-start
  7.2 0.0 all-reduce.5.cloned.1.call-start
  7.3 4.7 pad_slice_fusion.245
  11.9 3.3 copy.28
  15.3 2.5 collective-permute-start
  17.8 2.2 copy.31
  20.0 4.8 collective-permute-start.1
  25.0 0.0 copy-done.14
  25.0 0.0 copy-done.15
  25.1 1.8 pad.10
  26.9 0.0 collective-permute-done
  26.9 3.1 copy.29
  30.0 0.0 collective-permute-done.1
  30.0 3.0 copy.32
  33.0 83.0 %fusion.313 = (f32[96,128]{1,0:T(8,128)S(1)}, f32[96,96,128]{2,1,0:T(8,128)}) fusion(f32[96]{0:T(128)S(1)} %get-tuple-element.115, bf16[102,96,3]{2,1,0:T(8,128)(2,1)} %copy.32, bf16[102,96,128]{2,1,0:T(8,128)(2,1)S(1)} %pad.10, f32[96]{0:T(128)S(1)} %get-tuple-element.116, f32[96]{0:T(128)S(1)} %get-tuple-element.117, f32[96]{0:T(128)S(1)} %get-tuple-element.118, ...), kind=kLoop, calls=%fused_computation.718 | loop fusion | flops 322031616 | bytes 23932160 | tf_op jit(solution)/shard_map/reduce_sum | solution.py:37
  116.0 0.0 copy-start.3
  116.0 0.0 copy-start.16
  116.0 0.0 copy-start.17
  116.0 3.6 multiply_reduce_fusion.2
  119.6 10.9 %fusion.61 = bf16[96,96,128]{2,1,0:T(8,128)(2,1)} fusion(f32[96]{0:T(128)S(1)} %get-tuple-element.169, f32[96,96,128]{2,1,0:T(8,128)} %get-tuple-element.7, f32[96]{0:T(128)S(1)} %get-tuple-element.164, f32[96,128]{1,0:T(8,128)S(1)} %add_rsqrt_fusion.2, f32[96,128]{1,0:T(8,128)S(1)} %broadcast_multiply_fusion.2, bf16[2,384,96]{1,2,0:T(8,128)(2,1)S(1)} %copy-done.16, ...), kind=kOutput, calls=%fused_computation.304 | convolution fusion | flops 1863843840 | bytes 9683968 | tf_op jit(solution)/shard_map/lhw,hc->lcw/dot_general | solution.py:24
  130.5 4.6 pad_slice_fusion.243
  135.2 3.3 copy.34
  138.5 0.1 collective-permute-start.2
  138.6 2.2 copy.37
  140.8 5.1 %collective-permute-start.3 = (bf16[102,96,3]{0,1,2:T(8,128)(2,1)S(1)}, bf16[102,96,3]{0,1,2:T(8,128)(2,1)S(1)}, u32[]{:S(2)}, u32[]{:S(2)}) collective-permute-start(bf16[102,96,3]{0,1,2:T(8,128)(2,1)S(1)} %copy.37), channel_id=1, source_target_pairs={{1,0},{2,1},{3,2},{4,3},{5,4},{6,5},{7,6},{0,7},{9,8},{10,9},{11,1... | collective-permute-start | bytes 176264 | tf_op jit(solution)/shard_map/ppermute | solution.py:16
  146.0 1.8 pad.11
  147.8 0.0 collective-permute-done.2
  147.8 3.5 copy.35
  151.3 0.0 collective-permute-done.3
  151.3 3.0 copy.38
  154.3 82.9 %fusion.311 = (f32[96,128]{1,0:T(8,128)S(1)}, f32[96,96,128]{2,1,0:T(8,128)}) fusion(f32[96]{0:T(128)S(1)} %get-tuple-element.66, bf16[102,96,3]{2,1,0:T(8,128)(2,1)} %copy.38, bf16[102,96,128]{2,1,0:T(8,128)(2,1)S(1)} %pad.11, f32[96]{0:T(128)S(1)} %get-tuple-element.67, f32[96]{0:T(128)S(1)} %get-tuple-element.68, f32[96]{0:T(128)S(1)} %get-tuple-element.69, ...), kind=kLoop, calls=%fused_computation.717 | loop fusion | flops 322031616 | bytes 23932160 | tf_op jit(solution)/shard_map/reduce_sum | solution.py:37
  237.2 0.0 copy-start.4
  237.3 3.6 multiply_reduce_fusion.1
  240.9 0.0 copy-start.19
  240.9 10.9 %fusion.87 = bf16[96,96,128]{2,1,0:T(8,128)(2,1)} fusion(bf16[96,96,128]{2,1,0:T(8,128)(2,1)S(1)} %copy-done.4, f32[96]{0:T(128)S(1)} %get-tuple-element.170, f32[96,96,128]{2,1,0:T(8,128)} %get-tuple-element.5, f32[96]{0:T(128)S(1)} %get-tuple-element.163, f32[96,128]{1,0:T(8,128)S(1)} %add_rsqrt_fusion.1, f32[96,128]{1,0:T(8,128)S(1)} %broadcast_multiply_fusion.1, ...), kind=kOutput, calls=%fused_computation.330 | convolution fusion | flops 1863843840 | bytes 9683968 | tf_op jit(solution)/shard_map/lhw,hc->lcw/dot_general | solution.py:24
  251.7 0.0 copy-start.9
  251.7 0.0 copy-start.11
  251.8 0.0 copy-start.6
  251.8 3.4 fusion.267
  255.2 0.0 all-reduce.5.cloned.1.call-update
  255.3 117.9 %all-reduce.5.cloned.1.call-done = bf16[96,32,128]{2,1,0:T(8,128)(2,1)} async-done(((bf16[96,32,128]{2,1,0:T(8,128)(2,1)}), bf16[96,32,128]{2,1,0:T(8,128)(2,1)}) %all-reduce.5.cloned.1.call-update) | async-done | bytes 786448 | tf_op jit(solution)/shard_map/psum | solution.py:99
  373.2 2.0 fusion.271
  375.2 1.7 fusion.116
  376.9 1.4 copy-done.1
  378.3 2.3 pad_slice_fusion.241
  380.6 3.3 copy.40
  383.9 1.3 collective-permute-start.4
  385.3 2.2 copy.42
  387.5 3.9 collective-permute-start.5
  391.4 1.8 pad.12
  393.2 0.0 collective-permute-done.4
  393.2 3.3 copy.41
  396.5 0.0 collective-permute-done.5
  396.5 3.0 copy.43
  399.6 82.9 %fusion.309 = (f32[96,128]{1,0:T(8,128)S(1)}, f32[96,96,128]{2,1,0:T(8,128)}) fusion(f32[96]{0:T(128)S(1)} %get-tuple-element.63, bf16[102,96,3]{2,1,0:T(8,128)(2,1)} %copy.43, bf16[102,96,128]{2,1,0:T(8,128)(2,1)S(1)} %pad.12, f32[96]{0:T(128)S(1)} %get-tuple-element.64, f32[96]{0:T(128)S(1)} %get-tuple-element.17, f32[96]{0:T(128)S(1)} %get-tuple-element.18, ...), kind=kLoop, calls=%fused_computation.716 | loop fusion | flops 322031616 | bytes 23932160 | tf_op jit(solution)/shard_map/reduce_sum | solution.py:37
  482.5 0.0 copy-start.18
  482.5 0.0 copy-start.20
  482.5 0.0 copy-start.21
  482.5 3.6 multiply_reduce_fusion
  486.1 0.0 copy-start.12
  486.2 0.0 copy-start.13
  486.2 11.0 %fusion.114 = bf16[96,96,128]{2,1,0:T(8,128)(2,1)} fusion(bf16[96,96,128]{2,1,0:T(8,128)(2,1)S(1)} %copy-done.2, f32[96,128]{1,0:T(8,128)S(1)} %subtract_convert_fusion, f32[96]{0:T(128)S(1)} %copy-done.20, f32[96,96,128]{2,1,0:T(8,128)} %get-tuple-element.3, f32[96]{0:T(128)S(1)} %copy-done.21, f32[96,128]{1,0:T(8,128)S(1)} %add_rsqrt_fusion, ...), kind=kOutput, calls=%fused_computation.357 | convolution fusion | flops 1865023488 | bytes 9732864 | tf_op jit(solution)/shard_map/lhw,hc->lcw/dot_general | solution.py:24
  497.2 1.6 constant_dynamic-slice_fusion
  498.8 4.8 fusion.117
  (48 shorter events, 0.3 us)
Async XLA Ops:
  7.2 478.9 %copy-start = (bf16[384,96]{0,1:T(8,128)(2,1)S(1)}, bf16[384,96]{0,1:T(8,128)(2,1)}, u32[]{:S(2)}) copy-start(bf16[384,96]{0,1:T(8,128)(2,1)} %param.32) | copy-start | bytes 221188
  7.2 366.0 %all-reduce.5.cloned.1.call-start = ((), (), s32[]{:S(2)}) async-start(), calls=%async_computation | async-start | bytes 1572864 | tf_op jit(solution)/shard_map/psum | solution.py:99
  7.2 17.6 %copy-start.8 = (f32[2,7,7,96]{3,0,2,1:T(2,128)S(1)}, f32[2,7,7,96]{3,0,2,1:T(2,128)}, u32[]{:S(2)}) copy-start(f32[2,7,7,96]{3,0,2,1:T(2,128)} %param.22) | copy-start | bytes 112900
  7.2 17.8 %copy-start.14 = (f32[2,96]{1,0:T(2,128)S(1)}, f32[2,96]{1,0:T(2,128)}, u32[]{:S(2)}) copy-start(f32[2,96]{1,0:T(2,128)} %param.23) | copy-start | bytes 2308
  7.2 17.8 %copy-start.15 = (f32[2,96]{1,0:T(2,128)S(1)}, f32[2,96]{1,0:T(2,128)}, u32[]{:S(2)}) copy-start(f32[2,96]{1,0:T(2,128)} %param.26) | copy-start | bytes 2308
  15.3 11.6 %collective-permute-start = (bf16[102,96,3]{0,1,2:T(8,128)(2,1)S(1)}, bf16[102,96,3]{0,1,2:T(8,128)(2,1)S(1)}, u32[]{:S(2)}, u32[]{:S(2)}) collective-permute-start(bf16[102,96,3]{0,1,2:T(8,128)(2,1)S(1)} %copy.28), channel_id=1, source_target_pairs={{0,1},{1,2},{2,3},{3,4},{4,5},{5,6},{6,7},{7,0},{8,9},{9,10},{10,1... | collective-permute-start | bytes 176264 | tf_op jit(solution)/shard_map/ppermute | solution.py:14
  20.0 10.0 %collective-permute-start.1 = (bf16[102,96,3]{0,1,2:T(8,128)(2,1)S(1)}, bf16[102,96,3]{0,1,2:T(8,128)(2,1)S(1)}, u32[]{:S(2)}, u32[]{:S(2)}) collective-permute-start(bf16[102,96,3]{0,1,2:T(8,128)(2,1)S(1)} %copy.31), channel_id=1, source_target_pairs={{1,0},{2,1},{3,2},{4,3},{5,4},{6,5},{7,6},{0,7},{9,8},{10,9},{11,1... | collective-permute-start | bytes 176264 | tf_op jit(solution)/shard_map/ppermute | solution.py:16
  116.0 3.6 copy-start.3
  116.0 3.6 copy-start.16
  116.0 3.6 copy-start.17
  138.5 9.3 %collective-permute-start.2 = (bf16[102,96,3]{0,1,2:T(8,128)(2,1)S(1)}, bf16[102,96,3]{0,1,2:T(8,128)(2,1)S(1)}, u32[]{:S(2)}, u32[]{:S(2)}) collective-permute-start(bf16[102,96,3]{0,1,2:T(8,128)(2,1)S(1)} %copy.34), channel_id=1, source_target_pairs={{0,1},{1,2},{2,3},{3,4},{4,5},{5,6},{6,7},{7,0},{8,9},{9,10},{10,1... | collective-permute-start | bytes 176264 | tf_op jit(solution)/shard_map/ppermute | solution.py:14
  140.8 10.4 %collective-permute-start.3 = (bf16[102,96,3]{0,1,2:T(8,128)(2,1)S(1)}, bf16[102,96,3]{0,1,2:T(8,128)(2,1)S(1)}, u32[]{:S(2)}, u32[]{:S(2)}) collective-permute-start(bf16[102,96,3]{0,1,2:T(8,128)(2,1)S(1)} %copy.37), channel_id=1, source_target_pairs={{1,0},{2,1},{3,2},{4,3},{5,4},{6,5},{7,6},{0,7},{9,8},{10,9},{11,1... | collective-permute-start | bytes 176264 | tf_op jit(solution)/shard_map/ppermute | solution.py:16
  237.2 3.6 copy-start.4
  240.9 10.9 %copy-start.19 = (bf16[96,32]{0,1:T(8,128)(2,1)S(1)}, bf16[96,32]{0,1:T(8,128)(2,1)}, u32[]{:S(2)}) copy-start(bf16[96,32]{0,1:T(8,128)(2,1)} %param.27) | copy-start | bytes 18436
  251.7 3.5 copy-start.10
  251.7 3.5 copy-start.7
  251.7 3.6 copy-start.9
  251.7 121.4 %copy-start.11 = (bf16[2,32,96]{2,1,0:T(8,128)(2,1)S(1)}, bf16[2,32,96]{2,1,0:T(8,128)(2,1)}, u32[]{:S(2)}) copy-start(bf16[2,32,96]{2,1,0:T(8,128)(2,1)} %param.28) | copy-start | bytes 36868
  251.8 123.4 %copy-start.6 = (bf16[96,96,128]{2,1,0:T(8,128)(2,1)S(1)}, bf16[96,96,128]{2,1,0:T(8,128)(2,1)}, u32[]{:S(2)}) copy-start(bf16[96,96,128]{2,1,0:T(8,128)(2,1)} %param.19) | copy-start | bytes 7077892
  373.2 2.0 copy-start.5
  376.9 1.4 copy-start.1
  383.9 9.3 %collective-permute-start.4 = (bf16[102,96,3]{0,1,2:T(8,128)(2,1)S(1)}, bf16[102,96,3]{0,1,2:T(8,128)(2,1)S(1)}, u32[]{:S(2)}, u32[]{:S(2)}) collective-permute-start(bf16[102,96,3]{0,1,2:T(8,128)(2,1)S(1)} %copy.40), channel_id=1, source_target_pairs={{0,1},{1,2},{2,3},{3,4},{4,5},{5,6},{6,7},{7,0},{8,9},{9,10},{10,1... | collective-permute-start | bytes 176264 | tf_op jit(solution)/shard_map/ppermute | solution.py:14
  387.5 9.0 %collective-permute-start.5 = (bf16[102,96,3]{0,1,2:T(8,128)(2,1)S(1)}, bf16[102,96,3]{0,1,2:T(8,128)(2,1)S(1)}, u32[]{:S(2)}, u32[]{:S(2)}) collective-permute-start(bf16[102,96,3]{0,1,2:T(8,128)(2,1)S(1)} %copy.42), channel_id=1, source_target_pairs={{1,0},{2,1},{3,2},{4,3},{5,4},{6,5},{7,6},{0,7},{9,8},{10,9},{11,1... | collective-permute-start | bytes 176264 | tf_op jit(solution)/shard_map/ppermute | solution.py:16
  482.4 3.7 copy-start.2
  482.5 3.7 copy-start.18
  482.5 3.7 copy-start.20
  482.5 3.7 copy-start.21
  486.1 12.6 %copy-start.12 = (bf16[8,96]{1,0:T(8,128)(2,1)S(1)}, bf16[8,96]{1,0:T(8,128)(2,1)}, u32[]{:S(2)}) copy-start(bf16[8,96]{1,0:T(8,128)(2,1)} %param.35) | copy-start | bytes 4612
  486.2 12.6 %copy-start.13 = (bf16[96,8]{0,1:T(8,128)(2,1)S(1)}, bf16[96,8]{0,1:T(8,128)(2,1)}, u32[]{:S(2)}) copy-start(bf16[96,8]{0,1:T(8,128)(2,1)} %param.34) | copy-start | bytes 4612
Sparse Core Ops, SparseCore 0:
  255.3 117.8 all-reduce.4
where the time goes:
time: 514 us; the launch traced here: 511 us
  other arithmetic  260 us (51%)
  waiting for transfers between devices  118 us (23%)
  local copies, waits for them, and re-layouts  55.9 us (11%)
  matrix products  44.7 us (9%)
  starting transfers between devices  17.8 us (3%)
  between operations  14.9 us (3%)
    reduce_sum x3, other arithmetic, mixer(): center = acc - jnp.mean(acc, axis=1, keepdims=True)  249 us
    psum x1, waiting for transfers between devices, local(): flux_sum = lax.psum(flux.astype(jnp.bfloat16), 'member').astype(jnp.float32)  118 us
    dot_general x7, matrix products, contract(): return jnp.einsum(form, left.astype(jnp.float32), right.astype(jnp.float32))  44.7 us
    slice x6, local copies, waits for them, and re-layouts, with_halo(): lax.slice_in_dim(cells, cells.shape[dim] - width, cells.shape[dim], axis=...  21.6 us
    ppermute x3, starting transfers between devices, with_halo(): lax.ppermute(head, axis, [((i + 1) % count, i) for i in range(count)])  13.8 us
    reduce_sum x3, other arithmetic, mixer(): spread = jnp.mean(center * center, axis=1, keepdims=True)  10.7 us
  transfers between devices with their start and end apart: 7, of which 1 were waited for; matrix products, arithmetic and copies ran while one was open for 4% of the time, Pallas kernels for 0%

commit v1 on v0

v1 whole, which is shorter than its diff:
```python
import functools

import jax
import jax.numpy as jnp
from jax import lax
from jax.experimental import pallas as pl
from jax.experimental.pallas import tpu as pltpu
from jax.sharding import PartitionSpec as P

BF16 = jnp.bfloat16
F32 = jnp.float32
MESH = pl.DeviceIdType.MESH

C = 96
W = 128
LAT = 96
GROUP = 16
GROUPS = C // GROUP
OUT = 10
WIN = 16
PAIR = 2 * OUT
TILES = 5
SLOT = 6
TAPS = 7
DEPTH = TAPS * WIN * GROUP
ROWS_IN = 106
TANH_A = 2.0 * 0.7978845608028654
TANH_B = 8.0 * 0.7978845608028654 * 0.044715


def half_gelu(half):
    return half + half * jnp.tanh(half * (TANH_A + TANH_B * (half * half)))


def half_gelu_low(half):
    half = half.astype(BF16)
    return half + half * jnp.tanh(half * (BF16(TANH_A) + BF16(TANH_B) * (half * half)))


def lanes(shape):
    return lax.broadcasted_iota(jnp.int32, shape, len(shape) - 1)


def turn(v, shift):
    shift = shift % W
    return v if shift == 0 else pltpu.roll(v, shift, 1)


def band_matrix(kernel_of, taps, bands, outs):
    taps[...] = jnp.zeros(taps.shape, F32)
    for i in range(TAPS):
        taps[8 * i : 8 * i + TAPS, 0:C] = kernel_of(i)
    by_channel = jnp.transpose(taps[...])[0:C].astype(BF16)
    row = lax.broadcasted_iota(jnp.int32, (W, DEPTH), 0)
    lane = lanes((W, DEPTH))
    spread = (row % 8 == lane // (WIN * GROUP)) & (row // 8 == (lane % (WIN * GROUP)) // GROUP)
    wide = jnp.dot(by_channel, spread.astype(F32).astype(BF16), preferred_element_type=F32)
    crow = lax.broadcasted_iota(jnp.int32, (C, DEPTH), 0)
    wide = jnp.where(crow % GROUP == lanes((C, DEPTH)) % GROUP, wide, 0.0).astype(BF16)
    for g in range(GROUPS):
        base = wide[GROUP * g : GROUP * g + GROUP]
        for l in range(outs):
            bands[g, GROUP * l : GROUP * l + GROUP, :] = (
                base if l == 0 else pltpu.roll(base, GROUP * l, 1)
            )


def columns(vector_row):
    return jnp.transpose(jnp.broadcast_to(vector_row, (W, C)))


def shifted(cells, edge, d):
    if d == 0:
        return cells
    lane = lanes(cells.shape)
    if d > 0:
        return pltpu.roll(jnp.where(lane < d, edge, cells), W - d, 1)
    return pltpu.roll(jnp.where(lane >= W + d, edge, cells), -d, 1)


def conv_part(cells, edges, g, row):
    part = cells[pl.ds(row, WIN), GROUP * g : GROUP * g + GROUP, :].reshape(WIN * GROUP, W)
    edge = edges[pl.ds(row, WIN), GROUP * g : GROUP * g + GROUP, :].reshape(WIN * GROUP, W)
    return jnp.concatenate([shifted(part, edge, j - 3) for j in range(TAPS)], 0)


def conv_pair(cells, edges, bands, acc, row):
    for g in range(GROUPS):
        right = jnp.concatenate(
            [conv_part(cells, edges, g, row), conv_part(cells, edges, g, row + OUT)], 1
        )
        out = jnp.dot(bands[g], right, preferred_element_type=F32)
        for half in range(2):
            acc[OUT * half : OUT * half + OUT, GROUP * g : GROUP * g + GROUP, :] = out[
                :, half * W : half * W + W
            ].reshape(OUT, GROUP, W)


def normed(a, gain):
    center = a - jnp.mean(a, axis=0, keepdims=True)
    spread = jnp.mean(center * center, axis=0, keepdims=True)
    return (center * lax.rsqrt(spread + 1e-6) * gain).astype(BF16)


def branch(acc, count, up, down, gain):
    n = jnp.concatenate([normed(acc[k], gain) for k in range(count)], 1)
    hidden = half_gelu_low(jnp.dot(up, n, preferred_element_type=F32))
    return jnp.dot(down, hidden, preferred_element_type=F32)


def pack_edges(row_of, count):
    lane = lanes((C, W))
    slot = jnp.where(lane >= W - 3, 0, (lane + 3) // SLOT)
    packed = row_of(0)
    for k in range(1, count):
        packed = jnp.where(slot == k, turn(row_of(k), SLOT * k), packed)
    return packed


def joined_edges(from_left, from_right):
    lane = lanes((C, W))
    left_side = (lane >= W - 3) | ((lane < W - 5) & ((lane + 3) % SLOT < 3))
    return jnp.where(left_side, from_left, from_right)


def coupled_kernel(
    x_hbm, ocean_hbm, land, icem, ak, ag, au, ad, asc, fw, fl, okn, og, ou, od, osc, sw,
    y_hbm, surf_out, ocean_out,
    xp, xe, yp, ye, y2, bands1, bands2, bands3, acc, taps, up_t, down_t, gains, scales,
    ups_o, fw_t, fl_t, sw_t,
    pack1, fl1, fr1, pack2, fl2, fr2, flux, fluxes, oc, mid, mide, opack, orow_lo, orow_hi, oedge,
    surf, surfs,
    in_sem, oc_sem, out_sem, s1, r1, s2, r2, fs, fr, os_, or_, ss, sr, o_sem,
):
    m = lax.axis_index("member")
    b = lax.axis_index("lon")
    members = 16
    bands = 8
    right = lax.rem(b + 1, bands)
    left = lax.rem(b + bands - 1, bands)
    above = lax.rem(m + members - 1, members)
    below = lax.rem(m + 1, members)

    barrier = pltpu.get_barrier_semaphore()
    for side in (left, right):
        for who in (above, m, below):
            pl.semaphore_signal(barrier, inc=1, device_id=(who, side), device_id_type=MESH)

    @pl.loop(1, members)
    def _(k):
        pl.semaphore_signal(
            barrier, inc=1, device_id=(lax.rem(m + k, members), b), device_id_type=MESH
        )

    def load(p, rows):
        return pltpu.make_async_copy(
            x_hbm.at[0, pl.ds(p * PAIR, rows)], xp.at[pl.ds(3 + p * PAIR, rows)], in_sem.at[p]
        )

    for p in range(TILES):
        load(p, min(PAIR, LAT - p * PAIR)).start()
    oc_copy = pltpu.make_async_copy(ocean_hbm.at[pl.ds(6 * m, 6)], oc, oc_sem)
    oc_copy.start()

    for ref in (xp, xe, yp, ye):
        ref[0:3] = jnp.zeros((3, C, W), BF16)
        ref[99:ROWS_IN] = jnp.zeros((ROWS_IN - 99, C, W), BF16)

    def sends(p, packed, from_left, from_right, ssem, rsem):
        return (
            pltpu.make_async_remote_copy(
                packed.at[p], from_left.at[p], ssem.at[0, p], rsem.at[0, p],
                device_id=(m, right), device_id_type=MESH,
            ),
            pltpu.make_async_remote_copy(
                packed.at[p], from_right.at[p], ssem.at[1, p], rsem.at[1, p],
                device_id=(m, left), device_id_type=MESH,
            ),
        )

    for p in range(TILES):
        load(p, min(PAIR, LAT - p * PAIR)).wait()
        pack1[p] = pack_edges(lambda k: xp[3 + p * PAIR + k], min(PAIR, LAT - p * PAIR))

    pl.semaphore_wait(barrier, members - 1 + 6)

    for p in range(TILES):
        for copy in sends(p, pack1, fl1, fr1, s1, r1):
            copy.start()

    band_matrix(lambda i: ak[0, i], taps, bands1, OUT)
    band_matrix(lambda i: ak[1, i], taps, bands2, OUT)
    band_matrix(lambda i: okn[i], taps, bands3, 6)
    for layer in range(2):
        up_t[layer] = (jnp.transpose(au[layer].astype(F32)) * 0.5).astype(BF16)
        down_t[layer] = jnp.transpose(ad[layer].astype(F32)).astype(BF16)
        gains[layer] = columns(ag[layer : layer + 1])
        scales[layer] = columns(asc[layer : layer + 1])
    up_t[2] = (jnp.transpose(ou[...].astype(F32)) * 0.5).astype(BF16)
    down_t[2] = jnp.transpose(od[...].astype(F32)).astype(BF16)
    gains[2] = columns(og[...])
    scales[2] = columns(osc[...])
    fw_t[...] = (jnp.transpose(fw[...].astype(F32)) * 0.5).astype(BF16)
    for s in range(2):
        fl_t[s] = jnp.transpose(fl[s].astype(F32)).astype(BF16)
    sw_t[...] = jnp.transpose(sw[...].astype(F32)).astype(BF16)

    def spread_edges(p, from_left, from_right, edges):
        both = joined_edges(from_left[p], from_right[p])
        for k in range(PAIR):
            edges[3 + p * PAIR + k] = turn(both, -SLOT * k)

    def arrive(p, packed, from_left, from_right, ssem, rsem, edges):
        for copy in sends(p, packed, from_left, from_right, ssem, rsem):
            copy.wait()
        spread_edges(p, from_left, from_right, edges)

        @pl.when(p == TILES - 1)
        def _():
            edges[99:ROWS_IN] = jnp.zeros((ROWS_IN - 99, C, W), BF16)

    arrive(0, pack1, fl1, fr1, s1, r1, xe)

    @pl.loop(0, TILES)
    def _(p):
        @pl.when(p < TILES - 1)
        def _():
            arrive(p + 1, pack1, fl1, fr1, s1, r1, xe)

        conv_pair(xp, xe, bands1, acc, p * PAIR)
        add = branch(acc, PAIR, up_t[0], down_t[0], gains[0])
        for k in range(PAIR):
            yp[3 + p * PAIR + k] = (
                xp[3 + p * PAIR + k].astype(F32) + scales[0] * add[:, k * W : k * W + W]
            ).astype(BF16)
        pack2[p] = pack_edges(lambda k: yp[3 + p * PAIR + k], PAIR)
        for copy in sends(p, pack2, fl2, fr2, s2, r2):
            copy.start()

    yp[99:ROWS_IN] = jnp.zeros((ROWS_IN - 99, C, W), BF16)

    def flux_copy(d):
        return pltpu.make_async_remote_copy(
            flux.at[pl.ds(6 * d, 6)], fluxes.at[m], fs.at[d], fr.at[m],
            device_id=(d, b), device_id_type=MESH,
        )

    def flux_arrival(k):
        return pltpu.make_async_remote_copy(
            flux.at[pl.ds(6 * k, 6)], fluxes.at[k], fs.at[k], fr.at[k],
            device_id=(k, b), device_id_type=MESH,
        )

    def store(p, rows):
        return pltpu.make_async_copy(
            y2.at[pl.ds(p * PAIR, rows)], y_hbm.at[pl.ds(p * PAIR, rows)], out_sem.at[p]
        )

    arrive(0, pack2, fl2, fr2, s2, r2, ye)

    @pl.loop(0, TILES)
    def _(p):
        @pl.when(p < TILES - 1)
        def _():
            arrive(p + 1, pack2, fl2, fr2, s2, r2, ye)

        conv_pair(yp, ye, bands2, acc, p * PAIR)
        add = branch(acc, PAIR, up_t[1], down_t[1], gains[1])
        rows = []
        for k in range(PAIR):
            rows.append(
                (
                    yp[3 + p * PAIR + k].astype(F32) + scales[1] * add[:, k * W : k * W + W]
                ).astype(BF16)
            )
            y2[p * PAIR + k] = rows[k]
        out = half_gelu(
            jnp.dot(fw_t[...], jnp.concatenate(rows, 1), preferred_element_type=F32)
        ).astype(BF16)
        for k in range(PAIR):
            flux[p * PAIR + k] = out[:, k * W : k * W + W]

        @pl.when(p < TILES - 1)
        def _():
            store(p, PAIR).start()

        @pl.when(p == TILES - 1)
        def _():
            store(p, LAT - PAIR * (TILES - 1)).start()

        last = jnp.minimum((PAIR * (p + 1)) // 6, members)

        @pl.loop((PAIR * p) // 6, last)
        def _(d):
            @pl.when(d != m)
            def _():
                flux_copy(d).start()

    fluxes[m] = flux[pl.ds(6 * m, 6)]

    @pl.loop(0, members)
    def _(k):
        @pl.when(k != m)
        def _():
            flux_arrival(k).wait_recv()

    total = fluxes[0].astype(F32)
    for k in range(1, members):
        total = total + fluxes[k].astype(F32)
    low = (total * (1.0 / members)).astype(BF16)
    low = jnp.concatenate([low[k] for k in range(6)], 1)
    open_term = jnp.dot(fl_t[0], low, preferred_element_type=F32)
    ice_term = jnp.dot(fl_t[1], low, preferred_element_type=F32)
    oc_copy.wait()
    mid[...] = jnp.zeros(mid.shape, BF16)
    mide[...] = jnp.zeros(mide.shape, BF16)
    for k in range(6):
        sea = (1 - land[pl.ds(6 * m + k, 1), :]).astype(F32)
        ice = icem[pl.ds(6 * m + k, 1), :].astype(F32)
        at = slice(k * W, k * W + W)
        forcing = sea * ((1.0 - ice) * open_term[:, at] + ice * ice_term[:, at])
        mid[3 + k] = (oc[k].astype(F32) + forcing).astype(BF16)
    opack[...] = pack_edges(lambda k: mid[3 + k], 6)

    def ocean_rows_up():
        return pltpu.make_async_remote_copy(
            mid.at[pl.ds(3, 3)], orow_hi, os_.at[0], or_.at[0],
            device_id=(above, b), device_id_type=MESH,
        )

    def ocean_rows_down():
        return pltpu.make_async_remote_copy(
            mid.at[pl.ds(6, 3)], orow_lo, os_.at[1], or_.at[1],
            device_id=(below, b), device_id_type=MESH,
        )

    def edge_copy(step, side):
        who = (above, m, below)[step + 1]
        return pltpu.make_async_remote_copy(
            opack, oedge.at[1 - step, side], os_.at[2 + 2 * (step + 1) + side],
            or_.at[2 + 2 * (1 - step) + side],
            device_id=(who, (right, left)[side]), device_id_type=MESH,
        )

    has_above = m > 0
    has_below = m < members - 1

    def guarded(flag, act):
        if flag is None:
            act()
        else:
            pl.when(flag)(act)

    guards = {-1: has_above, 0: None, 1: has_below}
    pl.when(has_above)(lambda: ocean_rows_up().start())
    pl.when(has_below)(lambda: ocean_rows_down().start())
    for step in (0, -1, 1):
        for side in range(2):
            guarded(guards[step], lambda: edge_copy(step, side).start())

    pl.when(has_below)(lambda: ocean_rows_up().wait_recv())
    pl.when(has_above)(lambda: ocean_rows_down().wait_recv())
    for step in (0, 1, -1):
        for side in range(2):
            guarded(guards[-step], lambda: edge_copy(step, side).wait_recv())

    for step, first, count, at in ((-1, 3, 3, 0), (0, 0, 6, 3), (1, 0, 3, 9)):
        def fill(step=step, first=first, count=count, at=at):
            both = joined_edges(oedge[step + 1, 0], oedge[step + 1, 1])
            for k in range(count):
                mide[at + k] = turn(both, -SLOT * (first + k))

        guarded(guards[step], fill)

    pl.when(has_above)(lambda: ocean_rows_up().wait_send())
    pl.when(has_below)(lambda: ocean_rows_down().wait_send())
    for step in (0, -1, 1):
        for side in range(2):
            guarded(guards[step], lambda: edge_copy(step, side).wait_send())

    @pl.when(has_above)
    def _():
        mid[0:3] = orow_lo[...]

    @pl.when(has_below)
    def _():
        mid[9:12] = orow_hi[...]

    for g in range(GROUPS):
        out = jnp.dot(bands3[g], conv_part(mid, mide, g, 0), preferred_element_type=F32)
        acc[0:6, GROUP * g : GROUP * g + GROUP, :] = out.reshape(6, GROUP, W)
    add = branch(acc, 6, up_t[2], down_t[2], gains[2])
    rows = []
    for k in range(6):
        sea = (1 - land[pl.ds(6 * m + k, 1), :]).astype(F32)
        new = ((mid[3 + k].astype(F32) + scales[2] * add[:, k * W : k * W + W]) * sea).astype(BF16)
        ocean_out[k] = new
        rows.append(new)
    top = jnp.dot(sw_t[...], jnp.concatenate(rows, 1), preferred_element_type=F32).astype(BF16)
    for k in range(6):
        surf[k] = top[:, k * W : k * W + W]

    def surf_copy(d):
        return pltpu.make_async_remote_copy(
            surf, surfs.at[m], ss.at[d], sr.at[m], device_id=(d, b), device_id_type=MESH
        )

    def surf_arrival(k):
        return pltpu.make_async_remote_copy(
            surf, surfs.at[k], ss.at[k], sr.at[k], device_id=(k, b), device_id_type=MESH
        )

    @pl.loop(1, members)
    def _(k):
        surf_copy(lax.rem(m + k, members)).start()

    surfs[m] = surf[...]

    @pl.loop(1, members)
    def _(k):
        surf_arrival(lax.rem(m + k, members)).wait_recv()

    surf_out[...] = surfs[...]

    @pl.loop(1, members)
    def _(k):
        surf_copy(lax.rem(m + k, members)).wait_send()
        flux_copy(lax.rem(m + k, members)).wait_send()

    for p in range(TILES):
        store(p, min(PAIR, LAT - p * PAIR)).wait()


def couple_kernel(y, surf, land, back, out):
    back_t = jnp.transpose(back[...].astype(F32)).astype(BF16)
    rows = y.shape[0]
    top = jnp.concatenate([surf[k] for k in range(rows)], 1)
    add = jnp.dot(back_t, top, preferred_element_type=F32)
    for k in range(rows):
        sea = (1 - land[k : k + 1, :]).astype(F32)
        out[0, k] = (y[k].astype(F32) + sea * add[:, k * W : k * W + W]).astype(BF16)


def local(
    atmos, ocean, land_mask, ice_mask, atm_kernel, atm_gain, atm_up, atm_down, atm_scale,
    flux_weight, flux_lift, ocn_kernel, ocn_gain, ocn_up, ocn_down, ocn_scale,
    surf_weight, back_weight,
):
    vmem = pl.BlockSpec(memory_space=pltpu.VMEM)
    hbm = pl.BlockSpec(memory_space=pl.ANY)
    dma = pltpu.SemaphoreType.DMA
    V = pltpu.VMEM
    field = V((ROWS_IN, C, W), BF16)
    packed = V((TILES, C, W), BF16)
    y, surface, ocean_rows = pl.pallas_call(
        coupled_kernel,
        out_shape=(
            jax.ShapeDtypeStruct((LAT, C, W), BF16),
            jax.ShapeDtypeStruct((16, 6, 8, W), BF16),
            jax.ShapeDtypeStruct((6, C, W), BF16),
        ),
        in_specs=[hbm, hbm] + [vmem] * 15,
        out_specs=(hbm, vmem, vmem),
        scratch_shapes=[
            field, field, field, field, V((TILES * PAIR, C, W), BF16),
            V((GROUPS, GROUP * OUT, DEPTH), BF16), V((GROUPS, GROUP * OUT, DEPTH), BF16),
            V((GROUPS, GROUP * 6, DEPTH), BF16),
            V((PAIR, C, W), F32), V((W, W), F32),
            V((3, 384, C), BF16), V((3, C, 384), BF16), V((3, C, W), F32), V((3, C, W), F32),
            V((8, W), F32), V((32, C), BF16), V((2, C, 32), BF16), V((8, C), BF16),
            packed, packed, packed, packed, packed, packed,
            V((TILES * PAIR, 32, W), BF16), V((16, 6, 32, W), BF16),
            V((6, C, W), BF16), V((WIN, C, W), BF16), V((WIN, C, W), BF16), V((C, W), BF16),
            V((3, C, W), BF16), V((3, C, W), BF16), V((3, 2, C, W), BF16),
            V((6, 8, W), BF16), V((16, 6, 8, W), BF16),
            dma((TILES,)), dma, dma((TILES,)),
            dma((2, TILES)), dma((2, TILES)), dma((2, TILES)), dma((2, TILES)),
            dma((16,)), dma((16,)), dma((8,)), dma((8,)), dma((16,)), dma((16,)), dma,
        ],
        compiler_params=pltpu.CompilerParams(
            collective_id=0, has_side_effects=True, vmem_limit_bytes=60 * 2**20
        ),
        name="coupled",
    )(
        atmos, ocean, land_mask, ice_mask, atm_kernel, atm_gain, atm_up, atm_down, atm_scale,
        flux_weight, flux_lift, ocn_kernel, ocn_gain.reshape(1, C), ocn_up, ocn_down,
        ocn_scale.reshape(1, C), surf_weight,
    )
    step = 16
    atmos_out = pl.pallas_call(
        couple_kernel,
        grid=(LAT // step,),
        out_shape=jax.ShapeDtypeStruct((1, LAT, C, W), BF16),
        in_specs=[
            pl.BlockSpec((step, C, W), lambda t: (t, 0, 0)),
            pl.BlockSpec((step, 8, W), lambda t: (t, 0, 0)),
            pl.BlockSpec((step, W), lambda t: (t, 0)),
            pl.BlockSpec((8, C), lambda t: (0, 0)),
        ],
        out_specs=pl.BlockSpec((1, step, C, W), lambda t: (0, t, 0, 0)),
        name="couple",
    )(y, surface.reshape(LAT, 8, W), land_mask, back_weight)
    return (atmos_out, ocean_rows)


def solution(mesh):
    in_specs = (
        P("member", None, None, "lon"),
        P(None, None, "lon"),
        P(None, "lon"),
        P(None, "lon"),
    ) + (P(),) * 14
    out_specs = (P("member", None, None, "lon"), P("member", None, "lon"))
    return jax.shard_map(local, mesh=mesh, in_specs=in_specs, out_specs=out_specs, check_vma=False)
```

time: 514 us -> 84 us (0.16)
  other arithmetic: 260 us -> 0 us
  waiting for transfers between devices: 118 us -> 0 us
  Pallas kernels: 0 us -> 74.7 us
  local copies, waits for them, and re-layouts: 55.9 us -> 8.22 us
  matrix products: 44.7 us -> 0 us
  starting transfers between devices: 17.8 us -> 0 us
  between operations: 14.9 us -> 0.65 us
    reduce_sum x6 -> x0, other arithmetic: 259 us -> none  [the longest x3 249 us: mixer(): center = acc - jnp.mean(acc, axis=1, keepdims=True)]
    psum x1 -> x0, waiting for transfers between devices: 118 us -> none  [local(): flux_sum = lax.psum(flux.astype(jnp.bfloat16), 'member').astype(jnp.float32)]
    pallas_call x0 -> x2, Pallas kernels: none -> 74.7 us  [the longest x1 68.9 us: local(): pl.pallas_call(coupled_kernel, out_shape=(jax.ShapeDtypeStruct((LAT, C, W...]
    dot_general x7 -> x0, matrix products: 44.7 us -> none  [contract(): return jnp.einsum(form, left.astype(jnp.float32), right.astype(jnp.float32))]
    slice x10 -> x0, local copies, waits for them, and re-layouts: 28.3 us -> none  [the longest x6 21.6 us: with_halo(): lax.slice_in_dim(cells, cells.shape[dim] - width, cells.shape[dim], axis=...]
    ppermute x6 -> x0, local copies, waits for them, and re-layouts: 18.9 us -> none  [the longest x3 9.81 us: with_halo(): lax.ppermute(tail, axis, [(i, (i + 1) % count) for i in range(count)])]
    ppermute x6 -> x0, starting transfers between devices: 17.8 us -> none  [the longest x3 13.8 us: with_halo(): lax.ppermute(head, axis, [((i + 1) % count, i) for i in range(count)])]
    unnamed x44 -> x8, local copies, waits for them, and re-layouts: 1.5 us -> 8.22 us
  transfers between devices with their start and end apart: 7 -> 0, of which waited for: 1 -> 0; matrix products, arithmetic and copies ran while one was open for 4% -> 0% of each run, Pallas kernels for 0% -> 0%
where the time goes in v1:
time: 84 us; the launch traced here: 83.5 us
  Pallas kernels  74.7 us (89%)
  local copies, waits for them, and re-layouts  8.22 us (10%)
    pallas_call x1, Pallas kernels, local(): pl.pallas_call(coupled_kernel, out_shape=(jax.ShapeDtypeStruct((LAT, C, W...  68.9 us
    unnamed x8, local copies, waits for them, and re-layouts  8.22 us
    pallas_call x1, Pallas kernels, local(): pl.pallas_call(couple_kernel, grid=(LAT // step,), out_shape=jax.ShapeDty...  5.72 us

profile of v1, /device:TPU:1, one launch (start us, length us, event | category | flops | bytes accessed | tf_op | source)
XLA Modules:
  0.0 83.5 jit_solution(2327636725646324194)
XLA Ops:
  0.6 1.4 %copy.22.fw = bf16[96,32]{1,0:T(8,128)(2,1)} copy(bf16[96,32]{0,1:T(8,128)(2,1)} %param.27) | data formatting | bytes 12288 | tf_op args[9]
  2.0 1.4 %copy.24.sw = bf16[96,8]{1,0:T(8,128)(2,1)} copy(bf16[96,8]{0,1:T(8,128)(2,1)} %param.34) | data formatting | bytes 3072 | tf_op args[16]
  3.4 1.4 %copy.20.ak = f32[2,7,7,96]{3,2,1,0:T(8,128)} copy(f32[2,7,7,96]{3,0,2,1:T(2,128)} %param.22) | data formatting | bytes 75264 | tf_op args[4]
  4.8 1.6 %copy.23.od = bf16[384,96]{1,0:T(8,128)(2,1)} copy(bf16[384,96]{0,1:T(8,128)(2,1)} %param.32) | data formatting | bytes 147456 | tf_op args[14]
  6.5 1.7 %copy.21.ad = bf16[2,384,96]{2,1,0:T(8,128)(2,1)} copy(bf16[2,384,96]{1,2,0:T(8,128)(2,1)} %param.25) | data formatting | bytes 294912 | tf_op args[7]
  8.2 68.9 %coupled.1 = (bf16[96,96,128]{2,1,0:T(8,128)(2,1)}, bf16[16,6,8,128]{3,2,1,0:T(8,128)(2,1)}, bf16[6,96,128]{2,1,0:T(8,128)(2,1)}) custom-call(bf16[1,96,96,128]{3,2,1,0:T(8,128)(2,1)} %x_hbm.1, bf16[96,96,128]{2,1,0:T(8,128)(2,1)} %ocean_hbm.1, s32[96,128]{1,0:T(8,128)} %land.3, s32[96,128]{1,0:T(8,128)} %icem.1, f32[2,7,7,96]{3,2,1,0:T(8,128)} %copy.20.ak, ...), custom_call_target="tpu_custom_call" | custom-call | tf_op jit(solution)/shard_map/coupled/pallas_call | solution.py:455
  77.1 0.0 copy-start
  77.1 5.7 %couple.1 = bf16[1,96,96,128]{3,2,1,0:T(8,128)(2,1)} custom-call(bf16[96,96,128]{2,1,0:T(8,128)(2,1)} %get-tuple-element.5.y, bf16[96,8,128]{2,1,0:T(8,128)(2,1)} %bitcast.3, s32[96,128]{1,0:T(8,128)} %land.3, bf16[8,96]{1,0:T(8,128)(2,1)} %back.1), custom_call_target="tpu_custom_call" | custom-call | tf_op jit(solution)/shard_map/couple/pallas_call | solution.py:490
  82.9 0.0 copy-done
  82.9 0.7 copy.26
Async XLA Ops:
  77.1 5.7 %copy-start = (bf16[6,96,128]{2,1,0:T(8,128)(2,1)S(1)}, bf16[6,96,128]{2,1,0:T(8,128)(2,1)}, u32[]{:S(2)}) copy-start(bf16[6,96,128]{2,1,0:T(8,128)(2,1)} %get-tuple-element.11) | copy-start | bytes 442372

commit v2 on v1

v2 whole, which is shorter than its diff:
```python
import jax
import jax.numpy as jnp
from jax import lax
from jax.experimental import pallas as pl
from jax.experimental.pallas import tpu as pltpu
from jax.sharding import PartitionSpec as P

BF16 = jnp.bfloat16
F32 = jnp.float32
MESH = pl.DeviceIdType.MESH

C = 96
W = 128
LAT = 96
GROUP = 16
GROUPS = C // GROUP
OUT = 10
WIN = 16
PAIR = 2 * OUT
TILES = 5
SLOT = 6
TAPS = 7
DEPTH = TAPS * WIN * GROUP
ROWS_IN = 106
TANH_A = 2.0 * 0.7978845608028654
TANH_B = 8.0 * 0.7978845608028654 * 0.044715


def half_gelu(half):
    return half + half * jnp.tanh(half * (TANH_A + TANH_B * (half * half)))


def half_gelu_low(half):
    half = half.astype(BF16)
    return half + half * jnp.tanh(half * (BF16(TANH_A) + BF16(TANH_B) * (half * half)))


def lanes(shape):
    return lax.broadcasted_iota(jnp.int32, shape, len(shape) - 1)


def turn(v, shift):
    shift = shift % W
    return v if shift == 0 else pltpu.roll(v, shift, 1)


def band_matrix(kernel_of, taps, bands, outs):
    taps[...] = jnp.zeros(taps.shape, F32)
    for i in range(TAPS):
        taps[8 * i : 8 * i + TAPS, 0:C] = kernel_of(i)
    by_channel = jnp.transpose(taps[...])[0:C].astype(BF16)
    row = lax.broadcasted_iota(jnp.int32, (W, DEPTH), 0)
    lane = lanes((W, DEPTH))
    spread = (row % 8 == lane // (WIN * GROUP)) & (row // 8 == (lane % (WIN * GROUP)) // GROUP)
    wide = jnp.dot(by_channel, spread.astype(F32).astype(BF16), preferred_element_type=F32)
    crow = lax.broadcasted_iota(jnp.int32, (C, DEPTH), 0)
    wide = jnp.where(crow % GROUP == lanes((C, DEPTH)) % GROUP, wide, 0.0).astype(BF16)
    for g in range(GROUPS):
        base = wide[GROUP * g : GROUP * g + GROUP]
        for l in range(outs):
            bands[g, GROUP * l : GROUP * l + GROUP, :] = (
                base if l == 0 else pltpu.roll(base, GROUP * l, 1)
            )


def columns(vector_row):
    return jnp.transpose(jnp.broadcast_to(vector_row, (W, C)))


def shifted(cells, edge, d):
    if d == 0:
        return cells
    lane = lanes(cells.shape)
    if d > 0:
        return pltpu.roll(jnp.where(lane < d, edge, cells), W - d, 1)
    return pltpu.roll(jnp.where(lane >= W + d, edge, cells), -d, 1)


def conv_part(cells, edges, g, row):
    part = cells[pl.ds(row, WIN), GROUP * g : GROUP * g + GROUP, :].reshape(WIN * GROUP, W)
    edge = edges[pl.ds(row, WIN), GROUP * g : GROUP * g + GROUP, :].reshape(WIN * GROUP, W)
    return jnp.concatenate([shifted(part, edge, j - 3) for j in range(TAPS)], 0)


def conv_group(cells, edges, bands, acc, row, g):
    right = jnp.concatenate(
        [conv_part(cells, edges, g, row), conv_part(cells, edges, g, row + OUT)], 1
    )
    out = jnp.dot(bands[g], right, preferred_element_type=F32)
    for half in range(2):
        acc[OUT * half : OUT * half + OUT, GROUP * g : GROUP * g + GROUP, :] = out[
            :, half * W : half * W + W
        ].reshape(OUT, GROUP, W)


def normed(a, gain):
    center = a - jnp.mean(a, axis=0, keepdims=True)
    spread = jnp.mean(center * center, axis=0, keepdims=True)
    return (center * lax.rsqrt(spread + 1e-6) * gain).astype(BF16)


def branch(acc, first, count, up, down, gain):
    n = jnp.concatenate([normed(acc[first + k], gain) for k in range(count)], 1)
    hidden = half_gelu_low(jnp.dot(up, n, preferred_element_type=F32))
    return jnp.dot(down, hidden, preferred_element_type=F32)


def pack_edges(row_of, count):
    lane = lanes((C, W))
    slot = jnp.where(lane >= W - 3, 0, (lane + 3) // SLOT)
    packed = row_of(0)
    for k in range(1, count):
        packed = jnp.where(slot == k, turn(row_of(k), SLOT * k), packed)
    return packed


def pack_thin(row_of, count, shift):
    slot = lanes((C, W)) // 3
    packed = turn(row_of(0), shift)
    for k in range(1, count):
        packed = jnp.where(slot == k, turn(row_of(k), 3 * k + shift), packed)
    return packed


def joined_edges(from_left, from_right):
    lane = lanes((C, W))
    left_side = (lane >= W - 3) | ((lane < W - 5) & ((lane + 3) % SLOT < 3))
    return jnp.where(left_side, from_left, from_right)


def coupled_kernel(
    x_hbm, ocean_hbm, land, icem, ak, ag, au, ad, asc, fw, fl, okn, og, ou, od, osc, sw, bw,
    out_hbm, ocean_out,
    xp, xe, yp, ye, y2, bands1, bands2, bands3, acc0, acc1, taps, up_t, down_t, gains, scales,
    fw_t, fl_t, sw_t, bw_t,
    pack_r, pack_l, fl1, fr1, pack2, fl2, fr2, flux, fluxes, oc, mid, mide, opack, orow_lo, orow_hi,
    oedge, surf, surfs,
    in_sem, oc_sem, out_sem, s1, r1, s2, r2, fs, fr, os_, or_, ss, sr,
):
    m = lax.axis_index("member")
    b = lax.axis_index("lon")
    members = 16
    bands = 8
    right = lax.rem(b + 1, bands)
    left = lax.rem(b + bands - 1, bands)
    above = lax.rem(m + members - 1, members)
    below = lax.rem(m + 1, members)

    barrier = pltpu.get_barrier_semaphore()
    for side in (left, right):
        for who in (above, m, below):
            pl.semaphore_signal(barrier, inc=1, device_id=(who, side), device_id_type=MESH)

    @pl.loop(1, members)
    def _(k):
        pl.semaphore_signal(
            barrier, inc=1, device_id=(lax.rem(m + k, members), b), device_id_type=MESH
        )

    thin = ((0, 40), (40, 40), (80, 16))

    def load(q):
        first, rows = thin[q]
        return pltpu.make_async_copy(
            x_hbm.at[0, pl.ds(first, rows)], xp.at[pl.ds(3 + first, rows)], in_sem.at[q]
        )

    for q in range(3):
        load(q).start()
    oc_copy = pltpu.make_async_copy(ocean_hbm.at[pl.ds(6 * m, 6)], oc, oc_sem)
    oc_copy.start()

    for ref in (xp, xe, yp, ye):
        ref[0:3] = jnp.zeros((3, C, W), BF16)
        ref[99:ROWS_IN] = jnp.zeros((ROWS_IN - 99, C, W), BF16)

    def thin_sends(q):
        return (
            pltpu.make_async_remote_copy(
                pack_r.at[q], fl1.at[q], s1.at[0, q], r1.at[0, q],
                device_id=(m, right), device_id_type=MESH,
            ),
            pltpu.make_async_remote_copy(
                pack_l.at[q], fr1.at[q], s1.at[1, q], r1.at[1, q],
                device_id=(m, left), device_id_type=MESH,
            ),
        )

    for q in range(3):
        load(q).wait()
        first, rows = thin[q]
        pack_r[q] = pack_thin(lambda k: xp[3 + first + k], rows, 3)
        pack_l[q] = pack_thin(lambda k: xp[3 + first + k], rows, 0)
        if q == 0:
            pl.semaphore_wait(barrier, members - 1 + 6)
        for copy in thin_sends(q):
            copy.start()

    band_matrix(lambda i: ak[i, :, 0], taps, bands1, OUT)
    for layer in range(2):
        up_t[layer] = (jnp.transpose(au[layer].astype(F32)) * 0.5).astype(BF16)
        down_t[layer] = ad[layer]
        gains[layer] = columns(ag[layer : layer + 1])
        scales[layer] = columns(asc[layer : layer + 1])
    up_t[2] = (jnp.transpose(ou[...].astype(F32)) * 0.5).astype(BF16)
    down_t[2] = od[...]
    gains[2] = columns(og[...])
    scales[2] = columns(osc[...])
    fw_t[...] = fw[...] * BF16(0.5)
    for s in range(2):
        fl_t[s] = jnp.transpose(fl[s].astype(F32)).astype(BF16)
    sw_t[...] = sw[...]
    bw_t[...] = jnp.transpose(bw[...].astype(F32)).astype(BF16)
    band_matrix(lambda i: ak[i, :, 1], taps, bands2, OUT)
    band_matrix(lambda i: okn[i], taps, bands3, 6)

    def thin_arrive(q):
        for copy in thin_sends(q):
            copy.wait()

    def thin_spread(p, q, odd):
        lane = lanes((C, W))
        for k in range(PAIR):
            at = 3 * (PAIR * odd + k)
            xe[3 + p * PAIR + k] = jnp.where(
                lane < W // 2, turn(fr1[q], -at), turn(fl1[q], -at - 3)
            )

    def sends(p):
        return (
            pltpu.make_async_remote_copy(
                pack2.at[p], fl2.at[p], s2.at[0, p], r2.at[0, p],
                device_id=(m, right), device_id_type=MESH,
            ),
            pltpu.make_async_remote_copy(
                pack2.at[p], fr2.at[p], s2.at[1, p], r2.at[1, p],
                device_id=(m, left), device_id_type=MESH,
            ),
        )

    def arrive(p):
        for copy in sends(p):
            copy.wait()
        both = joined_edges(fl2[p], fr2[p])
        for k in range(PAIR):
            ye[3 + p * PAIR + k] = turn(both, -SLOT * k)

    half = PAIR // 2

    def mlp_one(acc, p, c):
        add = branch(acc, c * half, half, up_t[0], down_t[0], gains[0])
        for k in range(half):
            row = 3 + p * PAIR + c * half + k
            yp[row] = (xp[row].astype(F32) + scales[0] * add[:, k * W : k * W + W]).astype(BF16)

    def mlp_two(acc, p, c):
        add = branch(acc, c * half, half, up_t[1], down_t[1], gains[1])
        rows = []
        for k in range(half):
            row = p * PAIR + c * half + k
            rows.append(
                (yp[3 + row].astype(F32) + scales[1] * add[:, k * W : k * W + W]).astype(BF16)
            )
            y2[row] = rows[k]
        out = half_gelu(
            jnp.dot(fw_t[...], jnp.concatenate(rows, 1), preferred_element_type=F32)
        ).astype(BF16)
        for k in range(half):
            flux[p * PAIR + c * half + k] = out[:, k * W : k * W + W]

    def finish_one(p):
        pack2[p] = pack_edges(lambda k: yp[3 + p * PAIR + k], PAIR)
        for copy in sends(p):
            copy.start()

    def flux_copy(piece):
        d = piece // 3
        return pltpu.make_async_remote_copy(
            flux.at[pl.ds(2 * piece, 2)], fluxes.at[m, pl.ds(2 * lax.rem(piece, 3), 2)],
            fs.at[d], fr.at[m], device_id=(d, b), device_id_type=MESH,
        )

    def flux_whole(k):
        return pltpu.make_async_remote_copy(
            flux.at[pl.ds(6 * k, 6)], fluxes.at[k], fs.at[k], fr.at[k],
            device_id=(k, b), device_id_type=MESH,
        )

    def finish_two(p):
        @pl.loop(half * p, jnp.minimum(half * p + half, 3 * members))
        def _(piece):
            @pl.when(piece // 3 != m)
            def _():
                flux_copy(piece).start()

    def step(mlp, acc, p, conv, next_acc, next_p):
        cells, edges, bands = conv
        for g in range(GROUPS):
            conv_group(cells, edges, bands, next_acc, next_p * PAIR, g)
            if g == 0:
                mlp(acc, p, 0)
            if g == 3:
                mlp(acc, p, 1)

    one = (xp, xe, bands1)
    two = (yp, ye, bands2)
    thin_arrive(0)
    thin_spread(0, 0, 0)
    thin_spread(1, 0, 1)
    for g in range(GROUPS):
        conv_group(*one, acc0, 0, g)

    @pl.loop(0, 2)
    def _(t):
        thin_arrive(t + 1)
        thin_spread(2 * t + 2, t + 1, 0)

        @pl.when(t == 1)
        def _():
            xe[99:ROWS_IN] = jnp.zeros((ROWS_IN - 99, C, W), BF16)

        step(mlp_one, acc0, 2 * t, one, acc1, 2 * t + 1)
        finish_one(2 * t)

        @pl.when(t == 0)
        def _():
            thin_spread(3, 1, 1)

        step(mlp_one, acc1, 2 * t + 1, one, acc0, 2 * t + 2)
        finish_one(2 * t + 1)

    kind = lax.rem(m, 3)
    start = (kind + 1) // 2
    stride = 1 - 2 * (kind // 2)

    def order(s):
        return lax.rem(start + stride * s + TILES, TILES)

    for p in range(3):
        arrive(p)
    step(mlp_one, acc0, TILES - 1, two, acc1, start)
    finish_one(TILES - 1)
    yp[99:ROWS_IN] = jnp.zeros((ROWS_IN - 99, C, W), BF16)

    @pl.loop(0, 2)
    def _(t):
        @pl.when(t == 0)
        def _():
            arrive(3)

        step(mlp_two, acc1, order(2 * t), two, acc0, order(2 * t + 1))
        finish_two(order(2 * t))

        @pl.when(t == 0)
        def _():
            arrive(4)
            ye[99:ROWS_IN] = jnp.zeros((ROWS_IN - 99, C, W), BF16)

        step(mlp_two, acc0, order(2 * t + 1), two, acc1, order(2 * t + 2))
        finish_two(order(2 * t + 1))

    for c in range(2):
        mlp_two(acc1, order(4), c)
    finish_two(order(4))

    fluxes[m] = flux[pl.ds(6 * m, 6)]

    @pl.loop(0, members)
    def _(k):
        @pl.when(k != m)
        def _():
            flux_whole(k).wait_recv()

    total = fluxes[0].astype(F32)
    for k in range(1, members):
        total = total + fluxes[k].astype(F32)
    low = (total * (1.0 / members)).astype(BF16)
    low = jnp.concatenate([low[k] for k in range(6)], 1)
    open_term = jnp.dot(fl_t[0], low, preferred_element_type=F32)
    ice_term = jnp.dot(fl_t[1], low, preferred_element_type=F32)
    oc_copy.wait()
    mid[...] = jnp.zeros(mid.shape, BF16)
    mide[...] = jnp.zeros(mide.shape, BF16)
    for k in range(6):
        sea = (1 - land[pl.ds(6 * m + k, 1), :]).astype(F32)
        ice = icem[pl.ds(6 * m + k, 1), :].astype(F32)
        at = slice(k * W, k * W + W)
        forcing = sea * ((1.0 - ice) * open_term[:, at] + ice * ice_term[:, at])
        mid[3 + k] = (oc[k].astype(F32) + forcing).astype(BF16)
    opack[...] = pack_edges(lambda k: mid[3 + k], 6)

    def ocean_rows_up():
        return pltpu.make_async_remote_copy(
            mid.at[pl.ds(3, 3)], orow_hi, os_.at[0], or_.at[0],
            device_id=(above, b), device_id_type=MESH,
        )

    def ocean_rows_down():
        return pltpu.make_async_remote_copy(
            mid.at[pl.ds(6, 3)], orow_lo, os_.at[1], or_.at[1],
            device_id=(below, b), device_id_type=MESH,
        )

    def edge_copy(step, side):
        who = (above, m, below)[step + 1]
        return pltpu.make_async_remote_copy(
            opack, oedge.at[1 - step, side], os_.at[2 + 2 * (step + 1) + side],
            or_.at[2 + 2 * (1 - step) + side],
            device_id=(who, (right, left)[side]), device_id_type=MESH,
        )

    has_above = m > 0
    has_below = m < members - 1

    def guarded(flag, act):
        if flag is None:
            act()
        else:
            pl.when(flag)(act)

    guards = {-1: has_above, 0: None, 1: has_below}
    pl.when(has_above)(lambda: ocean_rows_up().start())
    pl.when(has_below)(lambda: ocean_rows_down().start())
    for step in (0, -1, 1):
        for side in range(2):
            guarded(guards[step], lambda: edge_copy(step, side).start())

    pl.when(has_below)(lambda: ocean_rows_up().wait_recv())
    pl.when(has_above)(lambda: ocean_rows_down().wait_recv())
    for step in (0, 1, -1):
        for side in range(2):
            guarded(guards[-step], lambda: edge_copy(step, side).wait_recv())

    for step, first, count, at in ((-1, 3, 3, 0), (0, 0, 6, 3), (1, 0, 3, 9)):
        def fill(step=step, first=first, count=count, at=at):
            both = joined_edges(oedge[step + 1, 0], oedge[step + 1, 1])
            for k in range(count):
                mide[at + k] = turn(both, -SLOT * (first + k))

        guarded(guards[step], fill)

    pl.when(has_above)(lambda: ocean_rows_up().wait_send())
    pl.when(has_below)(lambda: ocean_rows_down().wait_send())
    for step in (0, -1, 1):
        for side in range(2):
            guarded(guards[step], lambda: edge_copy(step, side).wait_send())

    @pl.when(has_above)
    def _():
        mid[0:3] = orow_lo[...]

    @pl.when(has_below)
    def _():
        mid[9:12] = orow_hi[...]

    for g in range(GROUPS):
        out = jnp.dot(bands3[g], conv_part(mid, mide, g, 0), preferred_element_type=F32)
        acc0[0:6, GROUP * g : GROUP * g + GROUP, :] = out.reshape(6, GROUP, W)
    add = branch(acc0, 0, 6, up_t[2], down_t[2], gains[2])
    rows = []
    for k in range(6):
        sea = (1 - land[pl.ds(6 * m + k, 1), :]).astype(F32)
        new = ((mid[3 + k].astype(F32) + scales[2] * add[:, k * W : k * W + W]) * sea).astype(BF16)
        ocean_out[k] = new
        rows.append(new)
    top = jnp.dot(sw_t[...], jnp.concatenate(rows, 1), preferred_element_type=F32).astype(BF16)
    for k in range(6):
        surf[k] = top[:, k * W : k * W + W]

    mine = pl.ds(6 * m, 6)

    def surf_copy(d):
        return pltpu.make_async_remote_copy(
            surf, surfs.at[mine], ss.at[d], sr.at[m], device_id=(d, b), device_id_type=MESH
        )

    def surf_arrival(k):
        return pltpu.make_async_remote_copy(
            surf, surfs.at[pl.ds(6 * k, 6)], ss.at[k], sr.at[k],
            device_id=(k, b), device_id_type=MESH,
        )

    @pl.loop(1, members)
    def _(k):
        surf_copy(lax.rem(m + k, members)).start()

    surfs[mine] = surf[...]

    @pl.loop(1, members)
    def _(k):
        surf_arrival(lax.rem(m + k, members)).wait_recv()

    def store(t):
        return pltpu.make_async_copy(
            y2.at[pl.ds(16 * t, 16)], out_hbm.at[0, pl.ds(16 * t, 16)], out_sem.at[t]
        )

    @pl.loop(0, LAT // 16)
    def _(t):
        top = jnp.concatenate([surfs[16 * t + k] for k in range(16)], 1)
        add = jnp.dot(bw_t[...], top, preferred_element_type=F32)
        for k in range(16):
            row = 16 * t + k
            sea = (1 - land[pl.ds(row, 1), :]).astype(F32)
            y2[row] = (y2[row].astype(F32) + sea * add[:, k * W : k * W + W]).astype(BF16)
        store(t).start()

    @pl.loop(1, members)
    def _(k):
        surf_copy(lax.rem(m + k, members)).wait_send()
        flux_whole(lax.rem(m + k, members)).wait_send()

    @pl.loop(0, LAT // 16)
    def _(t):
        store(t).wait()


def local(
    atmos, ocean, land_mask, ice_mask, atm_kernel, atm_gain, atm_up, atm_down, atm_scale,
    flux_weight, flux_lift, ocn_kernel, ocn_gain, ocn_up, ocn_down, ocn_scale,
    surf_weight, back_weight,
):
    vmem = pl.BlockSpec(memory_space=pltpu.VMEM)
    hbm = pl.BlockSpec(memory_space=pl.ANY)
    dma = pltpu.SemaphoreType.DMA
    V = pltpu.VMEM
    field = V((ROWS_IN, C, W), BF16)
    packed = V((TILES, C, W), BF16)
    thin = V((3, C, W), BF16)
    return pl.pallas_call(
        coupled_kernel,
        out_shape=(
            jax.ShapeDtypeStruct((1, LAT, C, W), BF16),
            jax.ShapeDtypeStruct((6, C, W), BF16),
        ),
        in_specs=[hbm, hbm] + [vmem] * 16,
        out_specs=(hbm, vmem),
        scratch_shapes=[
            field, field, field, field, V((TILES * PAIR, C, W), BF16),
            V((GROUPS, GROUP * OUT, DEPTH), BF16), V((GROUPS, GROUP * OUT, DEPTH), BF16),
            V((GROUPS, GROUP * 6, DEPTH), BF16),
            V((PAIR, C, W), F32), V((PAIR, C, W), F32), V((W, W), F32),
            V((3, 384, C), BF16), V((3, C, 384), BF16), V((3, C, W), F32), V((3, C, W), F32),
            V((32, C), BF16), V((2, C, 32), BF16), V((8, C), BF16), V((C, 8), BF16),
            thin, thin, thin, thin, packed, packed, packed,
            V((TILES * PAIR, 32, W), BF16), V((16, 6, 32, W), BF16),
            V((6, C, W), BF16), V((WIN, C, W), BF16), V((WIN, C, W), BF16), V((C, W), BF16),
            V((3, C, W), BF16), V((3, C, W), BF16), V((3, 2, C, W), BF16),
            V((6, 8, W), BF16), V((LAT, 8, W), BF16),
            dma((3,)), dma, dma((LAT // 16,)),
            dma((2, 3)), dma((2, 3)), dma((2, TILES)), dma((2, TILES)),
            dma((16,)), dma((16,)), dma((8,)), dma((8,)), dma((16,)), dma((16,)),
        ],
        compiler_params=pltpu.CompilerParams(
            collective_id=0, has_side_effects=True, vmem_limit_bytes=60 * 2**20
        ),
        name="coupled",
    )(
        atmos, ocean, land_mask, ice_mask, jnp.transpose(atm_kernel, (1, 2, 0, 3)), atm_gain,
        atm_up, jnp.swapaxes(atm_down, 1, 2), atm_scale, flux_weight.T, flux_lift, ocn_kernel,
        ocn_gain.reshape(1, C), ocn_up, ocn_down.T, ocn_scale.reshape(1, C), surf_weight.T,
        back_weight,
    )


def solution(mesh):
    in_specs = (
        P("member", None, None, "lon"),
        P(None, None, "lon"),
        P(None, "lon"),
        P(None, "lon"),
    ) + (P(),) * 14
    out_specs = (P("member", None, None, "lon"), P("member", None, "lon"))
    return jax.shard_map(local, mesh=mesh, in_specs=in_specs, out_specs=out_specs, check_vma=False)
```

time: 84 us -> 73.4 us (0.87)
  Pallas kernels: 74.7 us -> 68.6 us
  local copies, waits for them, and re-layouts: 8.22 us -> 3.92 us
    pallas_call x2 -> x1, Pallas kernels: 74.7 us -> 68.6 us  [local(): pl.pallas_call(coupled_kernel, out_shape=(jax.ShapeDtypeStruct((1, LAT, C...]
    unnamed x8 -> x4, local copies, waits for them, and re-layouts: 8.22 us -> 3.92 us
where the time goes in v2:
time: 73.4 us; the launch traced here: 73.2 us
  Pallas kernels  68.6 us (93%)
  local copies, waits for them, and re-layouts  3.92 us (5%)
    pallas_call x1, Pallas kernels, local(): pl.pallas_call(coupled_kernel, out_shape=(jax.ShapeDtypeStruct((1, LAT, C...  68.6 us
    unnamed x4, local copies, waits for them, and re-layouts  3.92 us

profile of v2, /device:TPU:1, one launch (start us, length us, event | category | flops | bytes accessed | tf_op | source)
XLA Modules:
  0.0 73.2 jit_solution(2130839297954925291)
XLA Ops:
  0.6 68.6 %coupled.1 = (bf16[1,96,96,128]{3,2,1,0:T(8,128)(2,1)}, bf16[6,96,128]{2,1,0:T(8,128)(2,1)}) custom-call(bf16[1,96,96,128]{3,2,1,0:T(8,128)(2,1)} %x_hbm.1, bf16[96,96,128]{2,1,0:T(8,128)(2,1)} %ocean_hbm.1, s32[96,128]{1,0:T(8,128)} %land.1, s32[96,128]{1,0:T(8,128)} %icem.1, f32[7,7,2,96]{3,2,1,0:T(2,128)} %bitcast.9, f32[2,96]{1,0:T(2,128)} %ag.1, ...), custom_call_target="tpu_custom_call" | custom-call | tf_op jit(solution)/shard_map/coupled/pallas_call | solution.py:530
  69.2 0.0 copy-start
  69.2 3.3 %copy.22 = bf16[1,96,96,128]{3,2,1,0:T(8,128)(2,1)} copy(bf16[1,96,96,128]{3,2,1,0:T(8,128)(2,1)} %get-tuple-element.4) | data formatting | bytes 4718592
  72.5 0.0 copy-done
  72.5 0.7 copy.23
Async XLA Ops:
  69.2 3.3 %copy-start = (bf16[6,96,128]{2,1,0:T(8,128)(2,1)S(1)}, bf16[6,96,128]{2,1,0:T(8,128)(2,1)}, u32[]{:S(2)}) copy-start(bf16[6,96,128]{2,1,0:T(8,128)(2,1)} %get-tuple-element.5) | copy-start | bytes 442372

commit v3 on v2

--- a/solution.py
+++ b/solution.py
@@ -19,6 +19,7 @@
 PAIR = 2 * OUT
 TILES = 5
 SLOT = 6
+FOLD = 32
 TAPS = 7
 DEPTH = TAPS * WIN * GROUP
 ROWS_IN = 106
@@ -129,13 +130,15 @@
 
 
 def coupled_kernel(
-    x_hbm, ocean_hbm, land, icem, ak, ag, au, ad, asc, fw, fl, okn, og, ou, od, osc, sw, bw,
-    out_hbm, ocean_out,
+    x_hbm, ocean_hbm, land_h, icem_h, ak_h, ag_h, au_h, ad_h, asc_h, fw_h, fl_h, okn_h, og_h,
+    ou_h, od_h, osc_h, sw_h, bw_h,
+    out_hbm, ocean_hbm_out,
+    land, icem, ak, ag, au, ad, asc, fw, fl, okn, og, ou, od, osc, sw, bw, ocean_out,
     xp, xe, yp, ye, y2, bands1, bands2, bands3, acc0, acc1, taps, up_t, down_t, gains, scales,
     fw_t, fl_t, sw_t, bw_t,
-    pack_r, pack_l, fl1, fr1, pack2, fl2, fr2, flux, fluxes, oc, mid, mide, opack, orow_lo, orow_hi,
-    oedge, surf, surfs,
-    in_sem, oc_sem, out_sem, s1, r1, s2, r2, fs, fr, os_, or_, ss, sr,
+    pack_r, pack_l, fl1, fr1, pack2, fl2, fr2, flux, fluxes, oc, mid, mide, opack,
+    oedge, lowrows, low_lo, low_hi, surf, surfs,
+    in_sem, oc_sem, out_sem, w_sem, oo_sem, s1, r1, s2, r2, fs, fr, os_, or_, ss, sr,
 ):
     m = lax.axis_index("member")
     b = lax.axis_index("lon")
@@ -167,7 +170,16 @@
 
     for q in range(3):
         load(q).start()
-    oc_copy = pltpu.make_async_copy(ocean_hbm.at[pl.ds(6 * m, 6)], oc, oc_sem)
+    pairs = (
+        (ak_h, ak), (au_h, au), (ad_h, ad), (ag_h, ag), (asc_h, asc), (fw_h, fw), (fl_h, fl),
+        (okn_h, okn), (og_h, og), (ou_h, ou), (od_h, od), (osc_h, osc), (sw_h, sw), (bw_h, bw),
+        (land_h, land), (icem_h, icem),
+    )
+    small = [pltpu.make_async_copy(a, c, w_sem.at[i]) for i, (a, c) in enumerate(pairs)]
+    for copy in small:
+        copy.start()
+    base = jnp.minimum(jnp.maximum(6 * m - 3, 0), LAT - 12)
+    oc_copy = pltpu.make_async_copy(ocean_hbm.at[pl.ds(base, 12)], oc, oc_sem)
     oc_copy.start()
 
     for ref in (xp, xe, yp, ye):
@@ -196,6 +208,8 @@
         for copy in thin_sends(q):
             copy.start()
 
+    for copy in small:
+        copy.wait()
     band_matrix(lambda i: ak[i, :, 0], taps, bands1, OUT)
     for layer in range(2):
         up_t[layer] = (jnp.transpose(au[layer].astype(F32)) * 0.5).astype(BF16)
@@ -220,7 +234,7 @@
 
     def thin_spread(p, q, odd):
         lane = lanes((C, W))
-        for k in range(PAIR):
+        for k in range(min(PAIR, LAT - p * PAIR)):
             at = 3 * (PAIR * odd + k)
             xe[3 + p * PAIR + k] = jnp.where(
                 lane < W // 2, turn(fr1[q], -at), turn(fl1[q], -at - 3)
@@ -286,8 +300,8 @@
             device_id=(k, b), device_id_type=MESH,
         )
 
-    def finish_two(p):
-        @pl.loop(half * p, jnp.minimum(half * p + half, 3 * members))
+    def finish_two(p, first=0, count=half):
+        @pl.loop(half * p + first, jnp.minimum(half * p + first + count, 3 * members))
         def _(piece):
             @pl.when(piece // 3 != m)
             def _():
@@ -310,24 +324,14 @@
     for g in range(GROUPS):
         conv_group(*one, acc0, 0, g)
 
-    @pl.loop(0, 2)
-    def _(t):
-        thin_arrive(t + 1)
-        thin_spread(2 * t + 2, t + 1, 0)
-
-        @pl.when(t == 1)
-        def _():
-            xe[99:ROWS_IN] = jnp.zeros((ROWS_IN - 99, C, W), BF16)
-
-        step(mlp_one, acc0, 2 * t, one, acc1, 2 * t + 1)
-        finish_one(2 * t)
-
-        @pl.when(t == 0)
-        def _():
-            thin_spread(3, 1, 1)
-
-        step(mlp_one, acc1, 2 * t + 1, one, acc0, 2 * t + 2)
-        finish_one(2 * t + 1)
+    for p in range(TILES - 1):
+        if p % 2 == 0:
+            thin_arrive(p // 2 + 1)
+        if p + 2 < TILES:
+            thin_spread(p + 2, (p + 2) // 2, p % 2)
+        acc, next_acc = (acc0, acc1) if p % 2 == 0 else (acc1, acc0)
+        step(mlp_one, acc, p, one, next_acc, p + 1)
+        finish_one(p)
 
     kind = lax.rem(m, 3)
     start = (kind + 1) // 2
@@ -361,7 +365,7 @@
 
     for c in range(2):
         mlp_two(acc1, order(4), c)
-    finish_two(order(4))
+        finish_two(order(4), c * (half // 2), half // 2)
 
     fluxes[m] = flux[pl.ds(6 * m, 6)]
 
@@ -374,30 +378,17 @@
     total = fluxes[0].astype(F32)
     for k in range(1, members):
         total = total + fluxes[k].astype(F32)
-    low = (total * (1.0 / members)).astype(BF16)
-    low = jnp.concatenate([low[k] for k in range(6)], 1)
-    open_term = jnp.dot(fl_t[0], low, preferred_element_type=F32)
-    ice_term = jnp.dot(fl_t[1], low, preferred_element_type=F32)
-    oc_copy.wait()
-    mid[...] = jnp.zeros(mid.shape, BF16)
-    mide[...] = jnp.zeros(mide.shape, BF16)
-    for k in range(6):
-        sea = (1 - land[pl.ds(6 * m + k, 1), :]).astype(F32)
-        ice = icem[pl.ds(6 * m + k, 1), :].astype(F32)
-        at = slice(k * W, k * W + W)
-        forcing = sea * ((1.0 - ice) * open_term[:, at] + ice * ice_term[:, at])
-        mid[3 + k] = (oc[k].astype(F32) + forcing).astype(BF16)
-    opack[...] = pack_edges(lambda k: mid[3 + k], 6)
-
-    def ocean_rows_up():
-        return pltpu.make_async_remote_copy(
-            mid.at[pl.ds(3, 3)], orow_hi, os_.at[0], or_.at[0],
+    lowrows[...] = (total * (1.0 / members)).astype(BF16)
+
+    def rows_up():
+        return pltpu.make_async_remote_copy(
+            lowrows.at[pl.ds(0, 3)], low_hi, os_.at[0], or_.at[0],
             device_id=(above, b), device_id_type=MESH,
         )
 
-    def ocean_rows_down():
-        return pltpu.make_async_remote_copy(
-            mid.at[pl.ds(6, 3)], orow_lo, os_.at[1], or_.at[1],
+    def rows_down():
+        return pltpu.make_async_remote_copy(
+            lowrows.at[pl.ds(3, 3)], low_lo, os_.at[1], or_.at[1],
             device_id=(below, b), device_id_type=MESH,
         )
 
@@ -408,6 +399,19 @@
             or_.at[2 + 2 * (1 - step) + side],
             device_id=(who, (right, left)[side]), device_id_type=MESH,
         )
+
+    def force(low, first):
+        rows = len(low)
+        low = jnp.concatenate(low, 1)
+        open_term = jnp.dot(fl_t[0], low, preferred_element_type=F32)
+        ice_term = jnp.dot(fl_t[1], low, preferred_element_type=F32)
+        for k in range(rows):
+            row = 6 * m - 3 + first + k
+            sea = (1 - land[pl.ds(row, 1), :]).astype(F32)
+            ice = icem[pl.ds(row, 1), :].astype(F32)
+            at = slice(k * W, k * W + W)
+            forcing = sea * ((1.0 - ice) * open_term[:, at] + ice * ice_term[:, at])
+            mid[first + k] = (oc[row - base].astype(F32) + forcing).astype(BF16)
 
     has_above = m > 0
     has_below = m < members - 1
@@ -419,39 +423,46 @@
             pl.when(flag)(act)
 
     guards = {-1: has_above, 0: None, 1: has_below}
-    pl.when(has_above)(lambda: ocean_rows_up().start())
-    pl.when(has_below)(lambda: ocean_rows_down().start())
-    for step in (0, -1, 1):
+    pl.when(has_above)(lambda: rows_up().start())
+    pl.when(has_below)(lambda: rows_down().start())
+    oc_copy.wait()
+    mid[...] = jnp.zeros(mid.shape, BF16)
+    mide[...] = jnp.zeros(mide.shape, BF16)
+    force([lowrows[k] for k in range(6)], 3)
+    edge = pack_edges(lambda k: mid[3 + k], 6)
+    fold = turn(edge[0:FOLD], 3)
+    for third in range(1, 3):
+        fold = jnp.where(
+            lanes((FOLD, W)) < 36 * third, fold,
+            turn(edge[FOLD * third : FOLD * third + FOLD], 3 + 36 * third),
+        )
+    opack[...] = fold
+    for step in (-1, 1, 0):
         for side in range(2):
             guarded(guards[step], lambda: edge_copy(step, side).start())
 
-    pl.when(has_below)(lambda: ocean_rows_up().wait_recv())
-    pl.when(has_above)(lambda: ocean_rows_down().wait_recv())
-    for step in (0, 1, -1):
-        for side in range(2):
-            guarded(guards[-step], lambda: edge_copy(step, side).wait_recv())
-
-    for step, first, count, at in ((-1, 3, 3, 0), (0, 0, 6, 3), (1, 0, 3, 9)):
-        def fill(step=step, first=first, count=count, at=at):
-            both = joined_edges(oedge[step + 1, 0], oedge[step + 1, 1])
+    @pl.when(has_below)
+    def _():
+        rows_up().wait_recv()
+        force([low_hi[k] for k in range(3)], 9)
+
+    @pl.when(has_above)
+    def _():
+        rows_down().wait_recv()
+        force([low_lo[k] for k in range(3)], 0)
+
+    def unfold(packed):
+        return jnp.concatenate([turn(packed, -3 - 36 * third) for third in range(3)], 0)
+
+    for view, first, count, at in ((0, 0, 6, 3), (-1, 3, 3, 0), (1, 0, 3, 9)):
+        def fill(view=view, first=first, count=count, at=at):
+            for side in range(2):
+                edge_copy(-view, side).wait_recv()
+            both = joined_edges(unfold(oedge[view + 1, 0]), unfold(oedge[view + 1, 1]))
             for k in range(count):
                 mide[at + k] = turn(both, -SLOT * (first + k))
 
-        guarded(guards[step], fill)
-
-    pl.when(has_above)(lambda: ocean_rows_up().wait_send())
-    pl.when(has_below)(lambda: ocean_rows_down().wait_send())
-    for step in (0, -1, 1):
-        for side in range(2):
-            guarded(guards[step], lambda: edge_copy(step, side).wait_send())
-
-    @pl.when(has_above)
-    def _():
-        mid[0:3] = orow_lo[...]
-
-    @pl.when(has_below)
-    def _():
-        mid[9:12] = orow_hi[...]
+        guarded(guards[view], fill)
 
     for g in range(GROUPS):
         out = jnp.dot(bands3[g], conv_part(mid, mide, g, 0), preferred_element_type=F32)
@@ -490,6 +501,9 @@
     def _(k):
         surf_arrival(lax.rem(m + k, members)).wait_recv()
 
+    ocean_store = pltpu.make_async_copy(ocean_out, ocean_hbm_out, oo_sem)
+    ocean_store.start()
+
     def store(t):
         return pltpu.make_async_copy(
             y2.at[pl.ds(16 * t, 16)], out_hbm.at[0, pl.ds(16 * t, 16)], out_sem.at[t]
@@ -505,6 +519,12 @@
             y2[row] = (y2[row].astype(F32) + sea * add[:, k * W : k * W + W]).astype(BF16)
         store(t).start()
 
+    pl.when(has_above)(lambda: rows_up().wait_send())
+    pl.when(has_below)(lambda: rows_down().wait_send())
+    for step in (0, -1, 1):
+        for side in range(2):
+            guarded(guards[step], lambda: edge_copy(step, side).wait_send())
+
     @pl.loop(1, members)
     def _(k):
         surf_copy(lax.rem(m + k, members)).wait_send()
@@ -513,6 +533,8 @@
     @pl.loop(0, LAT // 16)
     def _(t):
         store(t).wait()
+
+    ocean_store.wait()
 
 
 def local(
@@ -520,22 +542,28 @@
     flux_weight, flux_lift, ocn_kernel, ocn_gain, ocn_up, ocn_down, ocn_scale,
     surf_weight, back_weight,
 ):
-    vmem = pl.BlockSpec(memory_space=pltpu.VMEM)
     hbm = pl.BlockSpec(memory_space=pl.ANY)
     dma = pltpu.SemaphoreType.DMA
     V = pltpu.VMEM
     field = V((ROWS_IN, C, W), BF16)
     packed = V((TILES, C, W), BF16)
     thin = V((3, C, W), BF16)
+    small = (
+        land_mask, ice_mask, jnp.transpose(atm_kernel, (1, 2, 0, 3)), atm_gain, atm_up,
+        jnp.swapaxes(atm_down, 1, 2), atm_scale, flux_weight.T, flux_lift, ocn_kernel,
+        ocn_gain.reshape(1, C), ocn_up, ocn_down.T, ocn_scale.reshape(1, C), surf_weight.T,
+        back_weight,
+    )
     return pl.pallas_call(
         coupled_kernel,
         out_shape=(
             jax.ShapeDtypeStruct((1, LAT, C, W), BF16),
             jax.ShapeDtypeStruct((6, C, W), BF16),
         ),
-        in_specs=[hbm, hbm] + [vmem] * 16,
-        out_specs=(hbm, vmem),
+        in_specs=[hbm] * 18,
+        out_specs=(hbm, hbm),
         scratch_shapes=[
+            *[V(a.shape, a.dtype) for a in small], V((6, C, W), BF16),
             field, field, field, field, V((TILES * PAIR, C, W), BF16),
             V((GROUPS, GROUP * OUT, DEPTH), BF16), V((GROUPS, GROUP * OUT, DEPTH), BF16),
             V((GROUPS, GROUP * 6, DEPTH), BF16),
@@ -544,10 +572,11 @@
             V((32, C), BF16), V((2, C, 32), BF16), V((8, C), BF16), V((C, 8), BF16),
             thin, thin, thin, thin, packed, packed, packed,
             V((TILES * PAIR, 32, W), BF16), V((16, 6, 32, W), BF16),
-            V((6, C, W), BF16), V((WIN, C, W), BF16), V((WIN, C, W), BF16), V((C, W), BF16),
-            V((3, C, W), BF16), V((3, C, W), BF16), V((3, 2, C, W), BF16),
+            V((12, C, W), BF16), V((WIN, C, W), BF16), V((WIN, C, W), BF16), V((FOLD, W), BF16),
+            V((3, 2, FOLD, W), BF16),
+            V((6, 32, W), BF16), V((3, 32, W), BF16), V((3, 32, W), BF16),
             V((6, 8, W), BF16), V((LAT, 8, W), BF16),
-            dma((3,)), dma, dma((LAT // 16,)),
+            dma((3,)), dma, dma((LAT // 16,)), dma((16,)), dma,
             dma((2, 3)), dma((2, 3)), dma((2, TILES)), dma((2, TILES)),
             dma((16,)), dma((16,)), dma((8,)), dma((8,)), dma((16,)), dma((16,)),
         ],
@@ -555,12 +584,7 @@
             collective_id=0, has_side_effects=True, vmem_limit_bytes=60 * 2**20
         ),
         name="coupled",
-    )(
-        atmos, ocean, land_mask, ice_mask, jnp.transpose(atm_kernel, (1, 2, 0, 3)), atm_gain,
-        atm_up, jnp.swapaxes(atm_down, 1, 2), atm_scale, flux_weight.T, flux_lift, ocn_kernel,
-        ocn_gain.reshape(1, C), ocn_up, ocn_down.T, ocn_scale.reshape(1, C), surf_weight.T,
-        back_weight,
-    )
+    )(atmos, ocean, *small)
 
 
 def solution(mesh):

time: 73.4 us -> 71.4 us (0.973)
  Pallas kernels: 68.6 us -> 66.7 us
    pallas_call x1, Pallas kernels: 68.6 us -> 66.7 us  [local(): pl.pallas_call(coupled_kernel, out_shape=(jax.ShapeDtypeStruct((1, LAT, C...]
where the time goes in v3:
time: 71.4 us; the launch traced here: 71.2 us
  Pallas kernels  66.7 us (93%)
  local copies, waits for them, and re-layouts  3.92 us (5%)
    pallas_call x1, Pallas kernels, local(): pl.pallas_call(coupled_kernel, out_shape=(jax.ShapeDtypeStruct((1, LAT, C...  66.7 us
    unnamed x4, local copies, waits for them, and re-layouts  3.92 us

profile of v3, /device:TPU:1, one launch (start us, length us, event | category | flops | bytes accessed | tf_op | source)
XLA Modules:
  0.0 71.2 jit_solution(11959999664436824210)
XLA Ops:
  0.6 66.7 %coupled.1 = (bf16[1,96,96,128]{3,2,1,0:T(8,128)(2,1)}, bf16[6,96,128]{2,1,0:T(8,128)(2,1)}) custom-call(bf16[1,96,96,128]{3,2,1,0:T(8,128)(2,1)} %x_hbm.1, bf16[96,96,128]{2,1,0:T(8,128)(2,1)} %ocean_hbm.1, s32[96,128]{1,0:T(8,128)} %land_h.1, s32[96,128]{1,0:T(8,128)} %icem_h.1, f32[7,7,2,96]{3,2,1,0:T(2,128)} %bitcast.9, f32[2,96]{1,0:T(2,128)} %ag_h.1, ...), custom_call_target="tpu_custom_call" | custom-call | tf_op jit(solution)/shard_map/coupled/pallas_call | solution.py:557
  67.3 0.0 copy-start
  67.3 3.3 %copy.22 = bf16[1,96,96,128]{3,2,1,0:T(8,128)(2,1)} copy(bf16[1,96,96,128]{3,2,1,0:T(8,128)(2,1)} %get-tuple-element.4) | data formatting | bytes 4718592
  70.6 0.0 copy-done
  70.6 0.7 copy.23
Async XLA Ops:
  67.3 3.3 %copy-start = (bf16[6,96,128]{2,1,0:T(8,128)(2,1)S(1)}, bf16[6,96,128]{2,1,0:T(8,128)(2,1)}, u32[]{:S(2)}) copy-start(bf16[6,96,128]{2,1,0:T(8,128)(2,1)} %get-tuple-element.5) | copy-start | bytes 442372

commit v4 on v3

--- a/solution.py
+++ b/solution.py
@@ -20,6 +20,7 @@
 TILES = 5
 SLOT = 6
 FOLD = 32
+CHUNK = 32
 TAPS = 7
 DEPTH = TAPS * WIN * GROUP
 ROWS_IN = 106
@@ -131,14 +132,14 @@
 
 def coupled_kernel(
     x_hbm, ocean_hbm, land_h, icem_h, ak_h, ag_h, au_h, ad_h, asc_h, fw_h, fl_h, okn_h, og_h,
-    ou_h, od_h, osc_h, sw_h, bw_h,
-    out_hbm, ocean_hbm_out,
-    land, icem, ak, ag, au, ad, asc, fw, fl, okn, og, ou, od, osc, sw, bw, ocean_out,
+    ou_h, od_h, osc_h, sw_h,
+    y_hbm, ocean_hbm_out, surf_hbm,
+    land, icem, ak, ag, au, ad, asc, fw, fl, okn, og, ou, od, osc, sw, ocean_out,
     xp, xe, yp, ye, y2, bands1, bands2, bands3, acc0, acc1, taps, up_t, down_t, gains, scales,
-    fw_t, fl_t, sw_t, bw_t,
+    fw_t, fl_t, sw_t,
     pack_r, pack_l, fl1, fr1, pack2, fl2, fr2, flux, fluxes, oc, mid, mide, opack,
     oedge, lowrows, low_lo, low_hi, surf, surfs,
-    in_sem, oc_sem, out_sem, w_sem, oo_sem, s1, r1, s2, r2, fs, fr, os_, or_, ss, sr,
+    in_sem, oc_sem, out_sem, w_sem, s1, r1, s2, r2, fs, fr, os_, or_, ss, sr,
 ):
     m = lax.axis_index("member")
     b = lax.axis_index("lon")
@@ -172,7 +173,7 @@
         load(q).start()
     pairs = (
         (ak_h, ak), (au_h, au), (ad_h, ad), (ag_h, ag), (asc_h, asc), (fw_h, fw), (fl_h, fl),
-        (okn_h, okn), (og_h, og), (ou_h, ou), (od_h, od), (osc_h, osc), (sw_h, sw), (bw_h, bw),
+        (okn_h, okn), (og_h, og), (ou_h, ou), (od_h, od), (osc_h, osc), (sw_h, sw),
         (land_h, land), (icem_h, icem),
     )
     small = [pltpu.make_async_copy(a, c, w_sem.at[i]) for i, (a, c) in enumerate(pairs)]
@@ -224,7 +225,6 @@
     for s in range(2):
         fl_t[s] = jnp.transpose(fl[s].astype(F32)).astype(BF16)
     sw_t[...] = sw[...]
-    bw_t[...] = jnp.transpose(bw[...].astype(F32)).astype(BF16)
     band_matrix(lambda i: ak[i, :, 1], taps, bands2, OUT)
     band_matrix(lambda i: okn[i], taps, bands3, 6)
 
@@ -367,6 +367,9 @@
         mlp_two(acc1, order(4), c)
         finish_two(order(4), c * (half // 2), half // 2)
 
+    y_store = pltpu.make_async_copy(y2.at[pl.ds(0, LAT)], y_hbm, out_sem.at[0])
+    y_store.start()
+
     fluxes[m] = flux[pl.ds(6 * m, 6)]
 
     @pl.loop(0, members)
@@ -478,6 +481,7 @@
     for k in range(6):
         surf[k] = top[:, k * W : k * W + W]
 
+    ocean_store = pltpu.make_async_copy(ocean_out, ocean_hbm_out, out_sem.at[1])
     mine = pl.ds(6 * m, 6)
 
     def surf_copy(d):
@@ -495,29 +499,15 @@
     def _(k):
         surf_copy(lax.rem(m + k, members)).start()
 
+    ocean_store.start()
     surfs[mine] = surf[...]
 
     @pl.loop(1, members)
     def _(k):
         surf_arrival(lax.rem(m + k, members)).wait_recv()
 
-    ocean_store = pltpu.make_async_copy(ocean_out, ocean_hbm_out, oo_sem)
-    ocean_store.start()
-
-    def store(t):
-        return pltpu.make_async_copy(
-            y2.at[pl.ds(16 * t, 16)], out_hbm.at[0, pl.ds(16 * t, 16)], out_sem.at[t]
-        )
-
-    @pl.loop(0, LAT // 16)
-    def _(t):
-        top = jnp.concatenate([surfs[16 * t + k] for k in range(16)], 1)
-        add = jnp.dot(bw_t[...], top, preferred_element_type=F32)
-        for k in range(16):
-            row = 16 * t + k
-            sea = (1 - land[pl.ds(row, 1), :]).astype(F32)
-            y2[row] = (y2[row].astype(F32) + sea * add[:, k * W : k * W + W]).astype(BF16)
-        store(t).start()
+    surf_store = pltpu.make_async_copy(surfs, surf_hbm, out_sem.at[2])
+    surf_store.start()
 
     pl.when(has_above)(lambda: rows_up().wait_send())
     pl.when(has_below)(lambda: rows_down().wait_send())
@@ -530,11 +520,55 @@
         surf_copy(lax.rem(m + k, members)).wait_send()
         flux_whole(lax.rem(m + k, members)).wait_send()
 
-    @pl.loop(0, LAT // 16)
-    def _(t):
+    y_store.wait()
+    ocean_store.wait()
+    surf_store.wait()
+
+
+def couple_kernel(
+    y_hbm, o_hbm, surf_hbm, land_hbm, back_hbm, out_hbm, o_out,
+    y, o, surf, land, back, y_sem, s_sem, o_sem, out_sem,
+):
+    n = LAT // CHUNK
+
+    def load(t):
+        return pltpu.make_async_copy(
+            y_hbm.at[pl.ds(CHUNK * t, CHUNK)], y.at[pl.ds(CHUNK * t, CHUNK)], y_sem.at[t]
+        )
+
+    def store(t):
+        return pltpu.make_async_copy(
+            y.at[pl.ds(CHUNK * t, CHUNK)], out_hbm.at[0, pl.ds(CHUNK * t, CHUNK)], out_sem.at[t]
+        )
+
+    small = [
+        pltpu.make_async_copy(a, c, s_sem.at[i])
+        for i, (a, c) in enumerate(((surf_hbm, surf), (land_hbm, land), (back_hbm, back)))
+    ]
+    for copy in small:
+        copy.start()
+    for t in range(n):
+        load(t).start()
+    o_in = pltpu.make_async_copy(o_hbm, o, o_sem.at[0])
+    o_in.start()
+    for copy in small:
+        copy.wait()
+    back_t = jnp.transpose(back[...].astype(F32)).astype(BF16)
+    for t in range(n):
+        load(t).wait()
+        top = jnp.concatenate([surf[CHUNK * t + k] for k in range(CHUNK)], 1)
+        add = jnp.dot(back_t, top, preferred_element_type=F32)
+        for k in range(CHUNK):
+            row = CHUNK * t + k
+            sea = (1 - land[row : row + 1, :]).astype(F32)
+            y[row] = (y[row].astype(F32) + sea * add[:, k * W : k * W + W]).astype(BF16)
+        store(t).start()
+    o_in.wait()
+    o_back = pltpu.make_async_copy(o, o_out, o_sem.at[1])
+    o_back.start()
+    for t in range(n):
         store(t).wait()
-
-    ocean_store.wait()
+    o_back.wait()
 
 
 def local(
@@ -552,16 +586,16 @@
         land_mask, ice_mask, jnp.transpose(atm_kernel, (1, 2, 0, 3)), atm_gain, atm_up,
         jnp.swapaxes(atm_down, 1, 2), atm_scale, flux_weight.T, flux_lift, ocn_kernel,
         ocn_gain.reshape(1, C), ocn_up, ocn_down.T, ocn_scale.reshape(1, C), surf_weight.T,
-        back_weight,
     )
-    return pl.pallas_call(
+    y, ocean_rows, surface = pl.pallas_call(
         coupled_kernel,
         out_shape=(
-            jax.ShapeDtypeStruct((1, LAT, C, W), BF16),
+            jax.ShapeDtypeStruct((LAT, C, W), BF16),
             jax.ShapeDtypeStruct((6, C, W), BF16),
+            jax.ShapeDtypeStruct((LAT, 8, W), BF16),
         ),
-        in_specs=[hbm] * 18,
-        out_specs=(hbm, hbm),
+        in_specs=[hbm] * 17,
+        out_specs=(hbm, hbm, hbm),
         scratch_shapes=[
             *[V(a.shape, a.dtype) for a in small], V((6, C, W), BF16),
             field, field, field, field, V((TILES * PAIR, C, W), BF16),
@@ -569,14 +603,14 @@
             V((GROUPS, GROUP * 6, DEPTH), BF16),
             V((PAIR, C, W), F32), V((PAIR, C, W), F32), V((W, W), F32),
             V((3, 384, C), BF16), V((3, C, 384), BF16), V((3, C, W), F32), V((3, C, W), F32),
-            V((32, C), BF16), V((2, C, 32), BF16), V((8, C), BF16), V((C, 8), BF16),
+            V((32, C), BF16), V((2, C, 32), BF16), V((8, C), BF16),
             thin, thin, thin, thin, packed, packed, packed,
             V((TILES * PAIR, 32, W), BF16), V((16, 6, 32, W), BF16),
             V((12, C, W), BF16), V((WIN, C, W), BF16), V((WIN, C, W), BF16), V((FOLD, W), BF16),
             V((3, 2, FOLD, W), BF16),
             V((6, 32, W), BF16), V((3, 32, W), BF16), V((3, 32, W), BF16),
             V((6, 8, W), BF16), V((LAT, 8, W), BF16),
-            dma((3,)), dma, dma((LAT // 16,)), dma((16,)), dma,
+            dma((3,)), dma, dma((3,)), dma((15,)),
             dma((2, 3)), dma((2, 3)), dma((2, TILES)), dma((2, TILES)),
             dma((16,)), dma((16,)), dma((8,)), dma((8,)), dma((16,)), dma((16,)),
         ],
@@ -585,6 +619,22 @@
         ),
         name="coupled",
     )(atmos, ocean, *small)
+    return pl.pallas_call(
+        couple_kernel,
+        out_shape=(
+            jax.ShapeDtypeStruct((1, LAT, C, W), BF16),
+            jax.ShapeDtypeStruct((6, C, W), BF16),
+        ),
+        in_specs=[hbm] * 5,
+        out_specs=(hbm, hbm),
+        scratch_shapes=[
+            V((LAT, C, W), BF16), V((6, C, W), BF16), V((LAT, 8, W), BF16),
+            V((LAT, W), jnp.int32), V((8, C), BF16),
+            dma((LAT // CHUNK,)), dma((3,)), dma((2,)), dma((LAT // CHUNK,)),
+        ],
+        compiler_params=pltpu.CompilerParams(vmem_limit_bytes=60 * 2**20),
+        name="couple",
+    )(y, ocean_rows, surface, land_mask, back_weight)
 
 
 def solution(mesh):

time: 71.4 us -> 69.7 us (0.976)
  local copies, waits for them, and re-layouts: 3.92 us -> 0 us
  Pallas kernels: 66.7 us -> 68.7 us
    unnamed x4 -> x0, local copies, waits for them, and re-layouts: 3.92 us -> none
    pallas_call x1 -> x2, Pallas kernels: 66.7 us -> 68.7 us  [the longest x1 65.3 us: local(): pl.pallas_call(coupled_kernel, out_shape=(jax.ShapeDtypeStruct((LAT, C, W...]
where the time goes in v4:
time: 69.7 us; the launch traced here: 69.5 us
  Pallas kernels  68.7 us (99%)
  between operations  0.83 us (1%)
    pallas_call x1, Pallas kernels, local(): pl.pallas_call(coupled_kernel, out_shape=(jax.ShapeDtypeStruct((LAT, C, W...  65.3 us
    pallas_call x1, Pallas kernels, local(): pl.pallas_call(couple_kernel, out_shape=(jax.ShapeDtypeStruct((1, LAT, C,...  3.39 us

profile of v4, /device:TPU:1, one launch (start us, length us, event | category | flops | bytes accessed | tf_op | source)
XLA Modules:
  0.0 69.5 jit_solution(2643158347467128924)
XLA Ops:
  0.6 65.3 %coupled.1 = (bf16[96,96,128]{2,1,0:T(8,128)(2,1)}, bf16[6,96,128]{2,1,0:T(8,128)(2,1)}, bf16[96,8,128]{2,1,0:T(8,128)(2,1)}) custom-call(bf16[1,96,96,128]{3,2,1,0:T(8,128)(2,1)} %x_hbm.1, bf16[96,96,128]{2,1,0:T(8,128)(2,1)} %ocean_hbm.1, s32[96,128]{1,0:T(8,128)} %land_hbm.1, s32[96,128]{1,0:T(8,128)} %icem_h.1, f32[7,7,2,96]{3,2,1,0:T(2,128)} %bitcast.9, ...), custom_call_target="tpu_custom_call" | custom-call | tf_op jit(solution)/shard_map/coupled/pallas_call | solution.py:590
  65.9 3.4 %couple.1 = (bf16[1,96,96,128]{3,2,1,0:T(8,128)(2,1)}, bf16[6,96,128]{2,1,0:T(8,128)(2,1)}) custom-call(bf16[96,96,128]{2,1,0:T(8,128)(2,1)} %get-tuple-element.5.y_hbm, bf16[6,96,128]{2,1,0:T(8,128)(2,1)} %get-tuple-element.6.o_hbm, bf16[96,8,128]{2,1,0:T(8,128)(2,1)} %get-tuple-element.7.surf_hbm, s32[96,128]{1,0:T(8,128)} %land_hbm.1, bf16[8,96]{1,0:T(8,128)(2,1)} %back_hbm.1), custom_call_target="tpu_custom_call" | custom-call | tf_op jit(solution)/shard_map/couple/pallas_call | solution.py:622

commit v5 on v4

--- a/solution.py
+++ b/solution.py
@@ -138,7 +138,7 @@
     xp, xe, yp, ye, y2, bands1, bands2, bands3, acc0, acc1, taps, up_t, down_t, gains, scales,
     fw_t, fl_t, sw_t,
     pack_r, pack_l, fl1, fr1, pack2, fl2, fr2, flux, fluxes, oc, mid, mide, opack,
-    oedge, lowrows, low_lo, low_hi, surf, surfs,
+    oedge, lowrows, low_lo, low_hi, surf,
     in_sem, oc_sem, out_sem, w_sem, s1, r1, s2, r2, fs, fr, os_, or_, ss, sr,
 ):
     m = lax.axis_index("member")
@@ -486,12 +486,12 @@
 
     def surf_copy(d):
         return pltpu.make_async_remote_copy(
-            surf, surfs.at[mine], ss.at[d], sr.at[m], device_id=(d, b), device_id_type=MESH
+            surf, surf_hbm.at[mine], ss.at[d], sr.at[m], device_id=(d, b), device_id_type=MESH
         )
 
     def surf_arrival(k):
         return pltpu.make_async_remote_copy(
-            surf, surfs.at[pl.ds(6 * k, 6)], ss.at[k], sr.at[k],
+            surf, surf_hbm.at[pl.ds(6 * k, 6)], ss.at[k], sr.at[k],
             device_id=(k, b), device_id_type=MESH,
         )
 
@@ -500,14 +500,12 @@
         surf_copy(lax.rem(m + k, members)).start()
 
     ocean_store.start()
-    surfs[mine] = surf[...]
+    surf_store = pltpu.make_async_copy(surf, surf_hbm.at[mine], out_sem.at[2])
+    surf_store.start()
 
     @pl.loop(1, members)
     def _(k):
         surf_arrival(lax.rem(m + k, members)).wait_recv()
-
-    surf_store = pltpu.make_async_copy(surfs, surf_hbm, out_sem.at[2])
-    surf_store.start()
 
     pl.when(has_above)(lambda: rows_up().wait_send())
     pl.when(has_below)(lambda: rows_down().wait_send())
@@ -609,7 +607,7 @@
             V((12, C, W), BF16), V((WIN, C, W), BF16), V((WIN, C, W), BF16), V((FOLD, W), BF16),
             V((3, 2, FOLD, W), BF16),
             V((6, 32, W), BF16), V((3, 32, W), BF16), V((3, 32, W), BF16),
-            V((6, 8, W), BF16), V((LAT, 8, W), BF16),
+            V((6, 8, W), BF16),
             dma((3,)), dma, dma((3,)), dma((15,)),
             dma((2, 3)), dma((2, 3)), dma((2, TILES)), dma((2, TILES)),
             dma((16,)), dma((16,)), dma((8,)), dma((8,)), dma((16,)), dma((16,)),

time: 69.7 us -> 69.3 us (level)
  no operation moved by 1% of the time
where the time goes in v5:
time: 69.3 us; the launch traced here: 69.2 us
  Pallas kernels  68.3 us (99%)
  between operations  0.83 us (1%)
    pallas_call x1, Pallas kernels, local(): pl.pallas_call(coupled_kernel, out_shape=(jax.ShapeDtypeStruct((LAT, C, W...  64.9 us
    pallas_call x1, Pallas kernels, local(): pl.pallas_call(couple_kernel, out_shape=(jax.ShapeDtypeStruct((1, LAT, C,...  3.39 us

profile of v5, /device:TPU:1, one launch (start us, length us, event | category | flops | bytes accessed | tf_op | source)
XLA Modules:
  0.0 69.2 jit_solution(2555684219483478311)
XLA Ops:
  0.6 64.9 %coupled.1 = (bf16[96,96,128]{2,1,0:T(8,128)(2,1)}, bf16[6,96,128]{2,1,0:T(8,128)(2,1)}, bf16[96,8,128]{2,1,0:T(8,128)(2,1)}) custom-call(bf16[1,96,96,128]{3,2,1,0:T(8,128)(2,1)} %x_hbm.1, bf16[96,96,128]{2,1,0:T(8,128)(2,1)} %ocean_hbm.1, s32[96,128]{1,0:T(8,128)} %land_hbm.1, s32[96,128]{1,0:T(8,128)} %icem_h.1, f32[7,7,2,96]{3,2,1,0:T(2,128)} %bitcast.9, ...), custom_call_target="tpu_custom_call" | custom-call | tf_op jit(solution)/shard_map/coupled/pallas_call | solution.py:588
  65.6 3.4 %couple.1 = (bf16[1,96,96,128]{3,2,1,0:T(8,128)(2,1)}, bf16[6,96,128]{2,1,0:T(8,128)(2,1)}) custom-call(bf16[96,96,128]{2,1,0:T(8,128)(2,1)} %get-tuple-element.5.y_hbm, bf16[6,96,128]{2,1,0:T(8,128)(2,1)} %get-tuple-element.6.o_hbm, bf16[96,8,128]{2,1,0:T(8,128)(2,1)} %get-tuple-element.7.surf_hbm, s32[96,128]{1,0:T(8,128)} %land_hbm.1, bf16[8,96]{1,0:T(8,128)(2,1)} %back_hbm.1), custom_call_target="tpu_custom_call" | custom-call | tf_op jit(solution)/shard_map/couple/pallas_call | solution.py:620
